TPU v7x, 32 devices: a whole 2x2x4 slice. The times are simulated.
32 devices in a mesh: gx: 4 (over y, core), gy: 2 (over x), gz: 4 (over z).
Axes of the slice: x: 2, y: 2, z: 4, core: 2. Of those that a mesh axis runs over, the one named last changes fastest.
Arguments:
- initial_hydraulic_head: float32 [1024, 128], P(('gx', 'gy', 'gz')), may hold values from -6 to 6
- well_discharge: float32 [1024, 128], P(('gx', 'gy', 'gz')), may hold values from -6 to 6
- local_facet_coupling: bfloat16 [1024, 128, 128], P(('gx', 'gy', 'gz')), may hold values from -0.25 to 0.25
- diagonal_capacity: float32 [1024, 128], P(('gx', 'gy', 'gz')), may hold values from 0.5 to 2
- crossing_permeability: float32 [1024, 4], P(('gx', 'gy', 'gz')), may hold values from 0.3 to 3
- crossing_partner_number: int32 [1024, 4], P(('gx', 'gy', 'gz')), may hold values from 0 to 255, as said below
- liquid_thermal_state: float32 [1024, 128], P(('gx', 'gy', 'gz')), may hold values from -6 to 6
- transfer_factor: float32 [1024, 128], P(('gx', 'gy', 'gz')), may hold values from 0.1 to 1
- host_voxel_number: int32 [1024, 128], P(('gx', 'gy', 'gz')), may hold values from 0 to 65535
- stone_thermal_state: float32 [64, 64, 512], P('gx', 'gy', 'gz'), may hold values from -6 to 6
- matrix_diffusivity: float32 [64, 64, 512], P('gx', 'gy', 'gz'), may hold values from 0.02 to 0.16
Outputs:
- updated_hydraulic_head: float32 [1024, 128], P(('gx', 'gy', 'gz'))
- diffused_thermal_state: float32 [64, 64, 512], P('gx', 'gy', 'gz')
Inputs may be any that keep to these rules, and one draw needn't show every extreme that they name: `crossing_partner_number`: coupling ids name blocks of devices with the same gz index: c // 32 is the index on gx+gy of the owning device and c % 32 the block on it. The 128 couplings of one device name the blocks of any one device of its group at most 32 times, and exactly 32 times for some device.
All inputs are finite; a program needn't handle non-finite values.
Results may differ from a plain program's by a relative error of at most 0.00053.
Values sent between devices are 32-bit elements; how exact they have to be, the bound alone decides.
No kernel may reach another device: no remote copies, remote signals or barrier semaphores. Data moves between devices by JAX's collectives and lax.ppermute only.
A program may use at most 64 MiB of HBM per device.

v0:
```python
import functools

import jax
import jax.numpy as jnp
from jax import lax
from jax.experimental import pallas as pl
from jax.experimental.pallas import tpu as pltpu
from jax.sharding import PartitionSpec as P


SWEEPS = 3
AXES = ("gx", "gy", "gz")
GROUP = ("gx", "gy")
F32 = jnp.float32
BF16 = jnp.bfloat16
HIGH = lax.Precision.HIGHEST


def call(body, out_shape, *args, scratch=(), hbm=0):
    vmem = pl.BlockSpec(memory_space=pltpu.VMEM)
    args = [pltpu.with_memory_space_constraint(x, pltpu.HBM) for x in args[:hbm]] + list(args[hbm:])
    return pl.pallas_call(
        body,
        out_shape=out_shape,
        in_specs=[pl.BlockSpec(memory_space=pltpu.HBM)] * hbm + [vmem] * (len(args) - hbm),
        scratch_shapes=scratch,
        compiler_params=pltpu.CompilerParams(vmem_limit_bytes=48 << 20),
    )(*args)


def sds(shape, dtype=F32):
    return jax.ShapeDtypeStruct(shape, dtype)


def iota(shape, dim):
    return lax.broadcasted_iota(jnp.int32, shape, dim)


def dot(a, b, ca, cb, precision=None):
    return lax.dot_general(
        a, b, (((ca,), (cb,)), ((), ())), precision=precision, preferred_element_type=F32
    )


def group_size():
    return lax.axis_size("gx") * lax.axis_size("gy")


def by_pairs():
    n = group_size()
    return n <= 8 and n & (n - 1) == 0 and lax.axis_size("gx") % 2 == 0


def swap(x, k):
    n = group_size()
    return lax.ppermute(x, GROUP, [(i, i ^ k) for i in range(n)])


def meet(x):
    if not by_pairs():
        return [lax.all_gather(x, GROUP, axis=0, tiled=True)]
    n = group_size()
    low = lax.axis_size("gy")
    slots = [None] * n
    slots[0] = x
    for k in range(n - 1, 0, -1):
        if not k & low:
            slots[k] = swap(x, k)
    for k in range(n):
        if not k & low:
            slots[k | low] = swap(slots[k], low)
    return slots


def pair_lists(count):
    first = [(i, i ^ 1 if (i ^ 1) < count else i) for i in range(count)]
    second = []
    for i in range(count):
        j = i + 1 if i % 2 else i - 1
        second.append((i, j if 0 <= j < count else i))
    return first, second


def rounds_of(axis):
    count = lax.axis_size(axis)
    return 0 if count == 1 else 1 if count == 2 else 2


def face_specs(shape, lead):
    nx, ny, nz = shape
    full = {"gx": (lead, ny, nz), "gy": (lead, nx, nz), "gz": (lead, nx * ny)}
    return [(axis, r, full[axis]) for axis in AXES for r in range(rounds_of(axis))]


def exchange(faces, specs):
    out = []
    for face, (axis, r, _) in zip(faces, specs):
        out.append(lax.ppermute(face, axis, pair_lists(lax.axis_size(axis))[r]))
    return out


def write_faces(refs, specs, fields):
    for ref, (axis, r, _) in zip(refs, specs):
        even = lax.axis_index(axis) % 2 == 0
        high = even if r == 0 else jnp.logical_not(even)
        for j, t in enumerate(fields):
            nx, ny, nz = t.shape
            if axis == "gx":
                ref[j] = jnp.where(high, t[nx - 1], t[0])
            elif axis == "gy":
                ref[j] = jnp.where(high, t[:, ny - 1, :], t[:, 0, :])
            else:
                lane = jnp.where(high, nz - 1, 0)
                pick = (iota((8, nz), 1) == lane).astype(F32)
                row = dot(pick, t.reshape(nx * ny, nz), 1, 1, HIGH)
                ref[j : j + 1, :] = row[0:1, :]


def read_ghosts(refs, specs, j):
    got = {axis: [] for axis in AXES}
    for ref, (axis, r, _) in zip(refs, specs):
        got[axis].append(ref[j : j + 1, :] if axis == "gz" else ref[j])
    ghosts = {}
    for axis in AXES:
        faces = got[axis]
        if not faces:
            ghosts[axis] = None
            continue
        index, count = lax.axis_index(axis), lax.axis_size(axis)
        even = index % 2 == 0
        zero = jnp.zeros_like(faces[0])
        second = faces[1] if len(faces) > 1 else zero
        low = jnp.where(even, second, faces[0])
        high = jnp.where(even, faces[0], second)
        low = jnp.where(index > 0, low, zero)
        high = jnp.where(index < count - 1, high, zero)
        ghosts[axis] = (low, high)
    return ghosts


def embed_z(pair, shape):
    nx, ny, nz = shape
    low, high = pair
    rows = jnp.concatenate([low, high, jnp.zeros((6, nx * ny), F32)], axis=0)
    lane = jnp.where(iota((8, nz), 0) == 0, 0, nz - 1)
    pick = ((iota((8, nz), 1) == lane) & (iota((8, nz), 0) < 2)).astype(F32)
    return dot(rows, pick, 0, 0, HIGH).reshape(shape)


def interior(t, c):
    shape = t.shape
    _, ny, nz = shape
    gain = jnp.zeros(shape, F32)
    weight = jnp.zeros(shape, F32)
    wx = 0.5 * (c[:-1] + c[1:])
    none = jnp.zeros((1, ny, nz), F32)
    w_low = jnp.concatenate([none, wx], axis=0)
    w_high = jnp.concatenate([wx, none], axis=0)
    t_low = jnp.concatenate([none, t[:-1]], axis=0)
    t_high = jnp.concatenate([t[1:], none], axis=0)
    gain = gain + w_low * t_low + w_high * t_high
    weight = weight + w_low + w_high
    for dim, n in ((1, ny), (2, nz)):
        at = iota(shape, dim)
        for shift, edge in ((1, 0), (n - 1, n - 1)):
            w = jnp.where(at == edge, 0.0, 0.5 * (c + pltpu.roll(c, shift, dim)))
            gain = gain + w * pltpu.roll(t, shift, dim)
            weight = weight + w
    return gain, weight


def shards(
    initial_hydraulic_head,
    well_discharge,
    local_facet_coupling,
    diagonal_capacity,
    crossing_permeability,
    crossing_partner_number,
    liquid_thermal_state,
    transfer_factor,
    host_voxel_number,
    stone_thermal_state,
    matrix_diffusivity,
):
    nb, links = crossing_partner_number.shape
    tri = initial_hydraulic_head.shape[1]
    shape = stone_thermal_state.shape
    nx, ny, nz = shape
    rows_n = nx * ny
    n = group_size()
    pairs = by_pairs()
    specs2 = face_specs(shape, 2)
    specs1 = face_specs(shape, 1)
    nf = len(specs1)
    blk = sds((nb, tri))
    slab = sds(shape)

    def pre(*refs):
        (ids_hbm, perm_hbm, diag_hbm, *hbm), refs = refs[:11], refs[11:]
        kept, refs = refs[: len(hbm)], refs[len(hbm) :]
        mix_ref, den_ref, inner_ref, *faces = refs[: 3 + nf]
        ids_ref, perm_ref, sems = refs[3 + nf :]
        copies = [
            pltpu.make_async_copy(src, dst, sems.at[i])
            for i, (src, dst) in enumerate(
                zip((ids_hbm, perm_hbm, diag_hbm, *hbm), (ids_ref, perm_ref, den_ref, *kept))
            )
        ]
        for copy in copies:
            copy.start()
        h_ref, a_ref, t_ref, c_ref = kept[:4]
        for copy in copies[:3]:
            copy.wait()
        me = lax.axis_index("gx") * lax.axis_size("gy") + lax.axis_index("gy")
        ids, perm = ids_ref[...], perm_ref[...]
        if pairs:
            ids = ids ^ (me * nb)
        at = iota((n * nb, nb), 0)
        mix = jnp.zeros((n * nb, nb), F32)
        for k in range(links):
            mix = mix + jnp.where(at == ids[k : k + 1, :], perm[k : k + 1, :], 0.0)
        mix_ref[...] = mix
        rows = jnp.concatenate([perm, jnp.zeros((-links % 8, nb), F32)], axis=0)
        den_ref[...] = den_ref[...] + dot(rows, jnp.ones((rows.shape[0], tri), F32), 0, 0, HIGH)
        copies[3].wait()
        copies[4].wait()
        inner_body(a_ref, h_ref, inner_ref)
        for copy in copies[5:]:
            copy.wait()
        write_faces(faces, specs2, (t_ref[...], c_ref[...]))

    def inner_body(a_ref, h_ref, o_ref):
        h = h_ref[...].astype(BF16)
        for b in range(nb):
            o_ref[b : b + 1, :] = dot(h[b : b + 1, :], a_ref[b], 1, 1)

    def inner_of(h):
        return call(inner_body, blk, a, h)

    def sweep_of(mix_ref, den_ref, w_ref, inner_ref, slot_refs):
        heads = [r[...] for r in slot_refs]
        heads = jnp.concatenate(heads, axis=0) if len(heads) > 1 else heads[0]
        across = dot(mix_ref[...], heads, 0, 0, HIGH)
        return (w_ref[...] + inner_ref[...] + across) / den_ref[...]

    def sweep(mix_ref, den_ref, w_ref, inner_ref, *rest):
        rest[-1][...] = sweep_of(mix_ref, den_ref, w_ref, inner_ref, rest[:-1])

    def gather(first, t_ref, hv_ref, liq_ref, tf_ref, q_ref, hot_ref):
        t = t_ref[...].reshape(rows_n, nz)
        hi = t.astype(BF16)
        lo = (t - hi.astype(F32)).astype(BF16)
        both = jnp.concatenate([hi, lo], axis=1)
        hv = hv_ref[...]
        step = 4
        half = hot_ref.shape[1] // tri
        for b in range(0, half, step):
            cell = jnp.concatenate([hv[first + i : first + i + 1, :] for i in range(b, b + step)], axis=1)
            width = step * tri
            hot = (iota((rows_n, width), 0) == cell // nz).astype(F32).astype(BF16)
            hot_ref[:, b * tri : b * tri + width] = hot
            rows = dot(both, hot, 0, 0)
            rows = rows[:nz] + rows[nz:]
            value = jnp.sum(jnp.where(iota((nz, width), 0) == cell % nz, rows, 0.0), axis=0, keepdims=True)
            for i in range(step):
                q_ref[b + i : b + i + 1, :] = value[:, i * tri : (i + 1) * tri]
        own = slice(first, first + half)
        q_ref[...] = tf_ref[own, :] * (liq_ref[own, :] - q_ref[...])

    def base(t_ref, c_ref, *rest):
        got, outs = rest[:nf], rest[nf:]
        u_ref, keep_ref, wx_ref, wy_ref, wz_ref = outs
        t, c = t_ref[...], c_ref[...]
        gt = read_ghosts(got, specs2, 0)
        gc = read_ghosts(got, specs2, 1)
        gain, weight = interior(t, c)
        zx = jnp.zeros((ny, nz), F32)
        zy = jnp.zeros((nx, nz), F32)
        cx = gc["gx"] or (zx, zx)
        cy = gc["gy"] or (zy, zy)
        wx_low, wx_high = 0.5 * (c[0] + cx[0]), 0.5 * (c[nx - 1] + cx[1])
        wy_low, wy_high = 0.5 * (c[:, 0, :] + cy[0]), 0.5 * (c[:, ny - 1, :] + cy[1])
        at = iota(shape, 2)
        cz = embed_z(gc["gz"], shape) if gc["gz"] else jnp.zeros(shape, F32)
        wz = jnp.where((at == 0) | (at == nz - 1), 0.5 * (c + cz), 0.0)
        wx_ref[0], wx_ref[1] = wx_low, wx_high
        wy_ref[0], wy_ref[1] = wy_low, wy_high
        wz_ref[...] = wz
        keep_ref[...] = 1.0 - weight - wz
        keep_ref[0] = keep_ref[0] - wx_low
        keep_ref[nx - 1] = keep_ref[nx - 1] - wx_high
        keep_ref[:, 0, :] = keep_ref[:, 0, :] - wy_low
        keep_ref[:, ny - 1, :] = keep_ref[:, ny - 1, :] - wy_high
        u_ref[...] = gain + t * keep_ref[...]
        add_ghosts(u_ref, gt, wx_ref, wy_ref, wz_ref)

    def add_ghosts(u_ref, ghosts, wx_ref, wy_ref, wz_ref):
        if ghosts["gz"]:
            u_ref[...] = u_ref[...] + wz_ref[...] * embed_z(ghosts["gz"], shape)
        if ghosts["gx"]:
            u_ref[0] = u_ref[0] + wx_ref[0] * ghosts["gx"][0]
            u_ref[nx - 1] = u_ref[nx - 1] + wx_ref[1] * ghosts["gx"][1]
        if ghosts["gy"]:
            u_ref[:, 0, :] = u_ref[:, 0, :] + wy_ref[0] * ghosts["gy"][0]
            u_ref[:, ny - 1, :] = u_ref[:, ny - 1, :] + wy_ref[1] * ghosts["gy"][1]

    def heat(mix_ref, den_ref, w_ref, inner_ref, q1_ref, q2_ref, hv_ref, hot1_ref, hot2_ref, u_ref, *rest):
        ns = len(rest) - 3 - nf - 1
        slots, outs, pick_ref = rest[:ns], rest[ns:-1], rest[-1]
        h_ref, f_ref, t_ref = outs[:3]
        h = sweep_of(mix_ref, den_ref, w_ref, inner_ref, slots)
        h_ref[...] = h
        q = jnp.concatenate([q1_ref[...], q2_ref[...]], axis=0)
        flux = q * jnp.sqrt(1.0 + h * h)
        hi = flux.astype(BF16).astype(F32)
        lo = flux - hi
        lane = hv_ref[...] % nz
        for b in range(nb):
            mask = iota((nz, tri), 0) == lane[b : b + 1, :]
            pick_ref[:nz, b * tri : (b + 1) * tri] = jnp.where(mask, hi[b : b + 1, :], 0.0).astype(BF16)
            pick_ref[nz:, b * tri : (b + 1) * tri] = jnp.where(mask, lo[b : b + 1, :], 0.0).astype(BF16)
        half = hot1_ref.shape[1]
        both = dot(hot1_ref[...], pick_ref[:, :half], 1, 1) + dot(hot2_ref[...], pick_ref[:, half:], 1, 1)
        f = (both[:, :nz] + both[:, nz:]).reshape(shape)
        f_ref[...] = f
        t = u_ref[...] + f
        t_ref[...] = t
        write_faces(outs[3:], specs1, (t,))

    def middle(t_ref, f_ref, c_ref, keep_ref, v_ref):
        t = t_ref[...]
        gain, _ = interior(t, c_ref[...])
        v_ref[...] = f_ref[...] + t * keep_ref[...] + gain

    def last(v_ref, wx_ref, wy_ref, wz_ref, *rest):
        got, o_ref = rest[:-1], rest[-1]
        o_ref[...] = v_ref[...]
        add_ghosts(o_ref, read_ghosts(got, specs1, 0), wx_ref, wy_ref, wz_ref)

    h = initial_hydraulic_head
    slots = meet(h)
    h, a, t, c, w, hv, liq, tf, mix, den, inner, *faces = call(
        pre,
        [blk, sds(local_facet_coupling.shape, BF16), slab, slab, blk, sds((nb, tri), jnp.int32), blk, blk]
        + [sds((n * nb, nb)), blk, blk]
        + [sds(s) for _, _, s in specs2],
        crossing_partner_number.T,
        crossing_permeability.T,
        diagonal_capacity,
        h,
        local_facet_coupling,
        stone_thermal_state,
        matrix_diffusivity,
        well_discharge,
        host_voxel_number,
        liquid_thermal_state,
        transfer_factor,
        scratch=[pltpu.VMEM((links, nb), jnp.int32), pltpu.VMEM((links, nb), F32), pltpu.SemaphoreType.DMA((11,))],
        hbm=11,
    )
    slots[0] = h if pairs else slots[0]
    got = exchange(faces, specs2)
    h = call(sweep, blk, mix, den, w, inner, *slots)
    half = nb // 2
    parts = []
    for i in range(2):
        parts.append(
            call(
                functools.partial(gather, i * half), (sds((half, tri)), sds((rows_n, half * tri), BF16)), t, hv, liq, tf
            )
        )
    (q1, hot1), (q2, hot2) = parts
    u, keep, wx, wy, wz = call(base, (slab, slab, sds((2, ny, nz)), sds((2, nx, nz)), slab), t, c, *got)
    for _ in range(SWEEPS - 2):
        slots = meet(h)
        inner = inner_of(h)
        h = call(sweep, blk, mix, den, w, inner, *slots)
    slots = meet(h)
    inner = inner_of(h)
    h, f, t, *faces = call(
        heat,
        [blk, slab, slab] + [sds(s) for _, _, s in specs1],
        mix,
        den,
        w,
        inner,
        q1,
        q2,
        hv,
        hot1,
        hot2,
        u,
        *slots,
        scratch=[pltpu.VMEM((2 * nz, nb * tri), BF16)],
    )
    got = exchange(faces, specs1)
    v = call(middle, slab, t, f, c, keep)
    out = call(last, slab, v, wx, wy, wz, *got)
    return (h, out)


def solution(mesh):
    block = P(AXES, None)
    rock = P(*AXES)
    in_specs = (block, block, P(AXES, None, None)) + (block,) * 6 + (rock, rock)

    return jax.shard_map(shards, mesh=mesh, in_specs=in_specs, out_specs=(block, rock), check_vma=False)
```

profile of v0, /device:TPU:9, one launch (start us, length us, event | category | flops | bytes accessed | tf_op | source)
XLA Modules:
  0.0 50.6 jit_solution(5801334672970597234)
XLA Ops:
  0.6 1.3 %collective-permute-start = (f32[32,128]{1,0:T(8,128)}, f32[32,128]{1,0:T(8,128)S(1)}, u32[]{:S(2)}, u32[]{:S(2)}) collective-permute-start(f32[32,128]{1,0:T(8,128)} %refs_3_.1), channel_id=1, source_target_pairs={{0,4},{4,0},{8,12},{12,8},{16,20},{20,16},{24,28},{28,24},{1,5},{5... | collective-permute-start | bytes 49160 | tf_op jit(solution)/shard_map/ppermute | solution.py:56
  1.9 1.2 %collective-permute-start.4 = (f32[32,128]{1,0:T(8,128)}, f32[32,128]{1,0:T(8,128)S(1)}, u32[]{:S(2)}, u32[]{:S(2)}) collective-permute-start(f32[32,128]{1,0:T(8,128)} %refs_3_.1), channel_id=1, source_target_pairs={{0,20},{4,16},{8,28},{12,24},{16,4},{20,0},{24,12},{28,8},{1,21},{... | collective-permute-start | bytes 49160 | tf_op jit(solution)/shard_map/ppermute | solution.py:56
  3.1 0.2 collective-permute-start.3
  3.3 1.5 %collective-permute-start.1 = (f32[32,128]{1,0:T(8,128)}, f32[32,128]{1,0:T(8,128)S(1)}, u32[]{:S(2)}, u32[]{:S(2)}) collective-permute-start(f32[32,128]{1,0:T(8,128)} %refs_3_.1), channel_id=1, source_target_pairs={{0,8},{4,12},{8,0},{12,4},{16,24},{20,28},{24,16},{28,20},{1,9},{5... | collective-permute-start | bytes 49160 | tf_op jit(solution)/shard_map/ppermute | solution.py:56
  4.9 0.0 collective-permute-done.rest_1_
  4.9 0.5 collective-permute-start.2
  5.3 0.4 collective-permute-done.4.rest_5_
  5.8 1.9 %collective-permute-start.6 = (f32[32,128]{1,0:T(8,128)S(1)}, f32[32,128]{1,0:T(8,128)S(1)}, u32[]{:S(2)}, u32[]{:S(2)}) collective-permute-start(f32[32,128]{1,0:T(8,128)S(1)} %collective-permute-done.4.rest_5_), channel_id=1, source_target_pairs={{0,8},{4,12},{8,0},{12,4},{16,24},{20,28},{24,16},{28,20},{1,9},{5... | collective-permute-start | bytes 49160 | tf_op jit(solution)/shard_map/ppermute | solution.py:56
  7.7 0.0 collective-permute-done.3.rest_4_
  7.7 0.6 %collective-permute-start.5 = (f32[32,128]{1,0:T(8,128)S(1)}, f32[32,128]{1,0:T(8,128)S(1)}, u32[]{:S(2)}, u32[]{:S(2)}) collective-permute-start(f32[32,128]{1,0:T(8,128)S(1)} %collective-permute-done.3.rest_4_), channel_id=1, source_target_pairs={{0,8},{4,12},{8,0},{12,4},{16,24},{20,28},{24,16},{28,20},{1,9},{5... | collective-permute-start | bytes 49160 | tf_op jit(solution)/shard_map/ppermute | solution.py:56
  8.3 3.0 %shard_map.122 = (f32[32,128]{1,0:T(8,128)S(1)}, bf16[32,128,128]{2,1,0:T(8,128)(2,1)S(1)}, f32[16,32,128]{2,1,0:T(8,128)S(1)}, f32[16,32,128]{2,1,0:T(8,128)S(1...) custom-call(s32[4,32]{1,0:T(4,128)} %bitcast.2, ...), custom_call_target="tpu_custom_call" | custom-call | tf_op jit(solution)/shard_map/pallas_call | solution.py:22
  11.3 0.0 collective-permute-done.1.rest_2_
  11.3 0.0 collective-permute-done.2.rest_3_
  11.3 0.0 collective-permute-done.6.rest_7_
  11.3 0.0 collective-permute-done.5.rest_6_
  11.4 0.2 shard_map.123.h_ref.rest_0_
  11.6 1.2 %collective-permute-start.11 = (f32[32,128]{1,0:T(8,128)S(1)}, f32[32,128]{1,0:T(8,128)S(1)}, u32[]{:S(2)}, u32[]{:S(2)}) collective-permute-start(f32[32,128]{1,0:T(8,128)S(1)} %shard_map.123.h_ref.rest_0_), channel_id=1, source_target_pairs={{0,20},{4,16},{8,28},{12,24},{16,4},{20,0},{24,12},{28,8},{1,21},{... | collective-permute-start | bytes 49160 | tf_op jit(solution)/shard_map/ppermute | solution.py:56
  12.8 1.2 %collective-permute-start.10 = (f32[32,128]{1,0:T(8,128)S(1)}, f32[32,128]{1,0:T(8,128)S(1)}, u32[]{:S(2)}, u32[]{:S(2)}) collective-permute-start(f32[32,128]{1,0:T(8,128)S(1)} %shard_map.123.h_ref.rest_0_), channel_id=1, source_target_pairs={{0,16},{4,20},{8,24},{12,28},{16,0},{20,4},{24,8},{28,12},{1,17},{... | collective-permute-start | bytes 49160 | tf_op jit(solution)/shard_map/ppermute | solution.py:56
  14.1 0.3 collective-permute-start.7
  14.3 0.8 %collective-permute-start.8 = (f32[32,128]{1,0:T(8,128)S(1)}, f32[32,128]{1,0:T(8,128)S(1)}, u32[]{:S(2)}, u32[]{:S(2)}) collective-permute-start(f32[32,128]{1,0:T(8,128)S(1)} %shard_map.123.h_ref.rest_0_), channel_id=1, source_target_pairs={{0,8},{4,12},{8,0},{12,4},{16,24},{20,28},{24,16},{28,20},{1,9},{5... | collective-permute-start | bytes 49160 | tf_op jit(solution)/shard_map/ppermute | solution.py:56
  15.2 1.1 %collective-permute-start.13 = (f32[32,128]{1,0:T(8,128)S(1)}, f32[32,128]{1,0:T(8,128)S(1)}, u32[]{:S(2)}, u32[]{:S(2)}) collective-permute-start(f32[32,128]{1,0:T(8,128)S(1)} %collective-permute-done.11.rest_5_), channel_id=1, source_target_pairs={{0,8},{4,12},{8,0},{12,4},{16,24},{20,28},{24,16},{28,20},{1,9},{5... | collective-permute-start | bytes 49160 | tf_op jit(solution)/shard_map/ppermute | solution.py:56
  16.3 0.0 collective-permute-done.10.rest_4_
  16.3 0.5 %collective-permute-start.12 = (f32[32,128]{1,0:T(8,128)S(1)}, f32[32,128]{1,0:T(8,128)S(1)}, u32[]{:S(2)}, u32[]{:S(2)}) collective-permute-start(f32[32,128]{1,0:T(8,128)S(1)} %collective-permute-done.10.rest_4_), channel_id=1, source_target_pairs={{0,8},{4,12},{8,0},{12,4},{16,24},{20,28},{24,16},{28,20},{1,9},{5... | collective-permute-start | bytes 49160 | tf_op jit(solution)/shard_map/ppermute | solution.py:56
  16.8 1.5 %collective-permute-start.9 = (f32[32,128]{1,0:T(8,128)S(1)}, f32[32,128]{1,0:T(8,128)S(1)}, u32[]{:S(2)}, u32[]{:S(2)}) collective-permute-start(f32[32,128]{1,0:T(8,128)S(1)} %collective-permute-done.7.rest_1_), channel_id=1, source_target_pairs={{0,8},{4,12},{8,0},{12,4},{16,24},{20,28},{24,16},{28,20},{1,9},{5... | collective-permute-start | bytes 49160 | tf_op jit(solution)/shard_map/ppermute | solution.py:56
  18.4 0.0 collective-permute-start.14
  18.4 0.0 collective-permute-done.8.rest_2_
  18.4 0.3 collective-permute-start.16
  18.6 0.0 collective-permute-done.13.rest_7_
  18.6 0.2 collective-permute-start.17
  18.8 4.3 %collective-permute-start.18 = (f32[2,512]{1,0:T(2,128)S(1)}, f32[2,512]{1,0:T(2,128)S(1)}, u32[]{:S(2)}, u32[]{:S(2)}) collective-permute-start(f32[2,512]{1,0:T(2,128)S(1)} %get-tuple-element.54), channel_id=1, source_target_pairs={{0,0},{1,2},{2,1},{3,3},{4,4},{5,6},{6,5},{7,7},{8,8},{9,10},{10,9... | collective-permute-start | bytes 12296 | tf_op jit(solution)/shard_map/ppermute | solution.py:98
  23.1 0.6 %shard_map.124.inner_ref = f32[32,128]{1,0:T(8,128)S(1)} custom-call(bf16[32,128,128]{2,1,0:T(8,128)(2,1)S(1)} %get-tuple-element.38.a_ref, f32[32,128]{1,0:T(8,128)S(1)} %shard_map.123.h_ref.rest_0_), custom_call_target="tpu_custom_call" | custom-call | tf_op jit(solution)/shard_map/pallas_call | solution.py:22
  23.8 0.0 collective-permute-done.9.rest_3_
  23.8 4.3 %collective-permute-start.15 = (f32[2,32,128]{2,1,0:T(8,128)S(1)}, f32[2,32,128]{2,1,0:T(8,128)S(1)}, u32[]{:S(2)}, u32[]{:S(2)}) collective-permute-start(f32[2,32,128]{2,1,0:T(8,128)S(1)} %get-tuple-element.51), channel_id=1, source_target_pairs={{0,0},{8,16},{16,8},{24,24},{1,1},{9,17},{17,9},{25,25},{2,2},{10,... | collective-permute-start | bytes 98312 | tf_op jit(solution)/shard_map/ppermute | solution.py:98
  28.1 0.2 shard_map.125.h_ref.rest_0_
  28.3 0.1 collective-permute-start.23
  28.4 0.0 collective-permute-done.18.rest_4_
  28.4 1.4 %collective-permute-start.22 = (f32[32,128]{1,0:T(8,128)S(1)}, f32[32,128]{1,0:T(8,128)S(1)}, u32[]{:S(2)}, u32[]{:S(2)}) collective-permute-start(f32[32,128]{1,0:T(8,128)S(1)} %shard_map.125.h_ref.rest_0_), channel_id=1, source_target_pairs={{0,16},{4,20},{8,24},{12,28},{16,0},{20,4},{24,8},{28,12},{1,17},{... | collective-permute-start | bytes 49160 | tf_op jit(solution)/shard_map/ppermute | solution.py:56
  29.9 0.0 collective-permute-done.16.rest_2_
  29.9 1.2 %collective-permute-start.19 = (f32[32,128]{1,0:T(8,128)S(1)}, f32[32,128]{1,0:T(8,128)S(1)}, u32[]{:S(2)}, u32[]{:S(2)}) collective-permute-start(f32[32,128]{1,0:T(8,128)S(1)} %shard_map.125.h_ref.rest_0_), channel_id=1, source_target_pairs={{0,4},{4,0},{8,12},{12,8},{16,20},{20,16},{24,28},{28,24},{1,5},{5... | collective-permute-start | bytes 49160 | tf_op jit(solution)/shard_map/ppermute | solution.py:56
  31.1 0.0 collective-permute-start.20
  31.1 0.8 %collective-permute-done.23.rest_5_ = f32[32,128]{1,0:T(8,128)S(1)} collective-permute-done((f32[32,128]{1,0:T(8,128)S(1)}, f32[32,128]{1,0:T(8,128)S(1)}, u32[]{:S(2)}, u32[]{:S(2)}) %collective-permute-start.23) | collective-permute-done | bytes 16416 | tf_op jit(solution)/shard_map/ppermute | solution.py:56
  31.9 0.0 collective-permute-start.25
  31.9 0.0 collective-permute-done.22.rest_4_
  31.9 0.9 %collective-permute-start.24 = (f32[32,128]{1,0:T(8,128)S(1)}, f32[32,128]{1,0:T(8,128)S(1)}, u32[]{:S(2)}, u32[]{:S(2)}) collective-permute-start(f32[32,128]{1,0:T(8,128)S(1)} %collective-permute-done.22.rest_4_), channel_id=1, source_target_pairs={{0,8},{4,12},{8,0},{12,4},{16,24},{20,28},{24,16},{28,20},{1,9},{5... | collective-permute-start | bytes 49160 | tf_op jit(solution)/shard_map/ppermute | solution.py:56
  32.8 0.0 collective-permute-done.19.rest_1_
  32.8 0.1 collective-permute-start.21
  32.9 1.2 %shard_map.128 = (f32[16,128]{1,0:T(8,128)S(1)}, bf16[512,2048]{1,0:T(8,128)(2,1)S(1)}) custom-call(f32[16,32,128]{2,1,0:T(8,128)S(1)} %get-tuple-element.41.t_ref, s32[32,128]{1,0:T(8,128)S(1)} %get-tuple-element.42.hv_ref, f32[32,128]{1,0:T(8,128)S(1)} %get-tuple-element.43.liq_ref, f32[32,128]{1,0:T(8,128)S(1)} %get-tuple-element.44.tf_ref), custom_call_target="tpu_custom_call" | custom-call | tf_op jit(solution)/shard_map/pallas_call | solution.py:22
  34.1 1.2 %shard_map.127 = (f32[16,128]{1,0:T(8,128)S(1)}, bf16[512,2048]{1,0:T(8,128)(2,1)S(1)}) custom-call(f32[16,32,128]{2,1,0:T(8,128)S(1)} %get-tuple-element.41.t_ref, s32[32,128]{1,0:T(8,128)S(1)} %get-tuple-element.42.hv_ref, f32[32,128]{1,0:T(8,128)S(1)} %get-tuple-element.43.liq_ref, f32[32,128]{1,0:T(8,128)S(1)} %get-tuple-element.44.tf_ref), custom_call_target="tpu_custom_call" | custom-call | tf_op jit(solution)/shard_map/pallas_call | solution.py:22
  35.3 0.9 %shard_map.129 = (f32[16,32,128]{2,1,0:T(8,128)S(1)}, f32[16,32,128]{2,1,0:T(8,128)S(1)}, f32[2,32,128]{2,1,0:T(8,128)S(1)}, f32[2,16,128]{2,1,0:T(8,128)S(1)}, f32[16,32,128]{2,1,0:T(8,128)S(1)}) custom-call(f32[16,32,128]{2,1,0:T(8,128)S(1)} %get-tuple-element.41.t_ref, f32[16,32,128]{2,1,0:T(8,128)S(1)} %get-tuple-element.49.c_ref, ...), custom_call_target="tpu_custom_call" | custom-call | tf_op jit(solution)/shard_map/pallas_call | solution.py:22
  36.2 0.6 %shard_map.126.inner_ref = f32[32,128]{1,0:T(8,128)S(1)} custom-call(bf16[32,128,128]{2,1,0:T(8,128)(2,1)S(1)} %get-tuple-element.38.a_ref, f32[32,128]{1,0:T(8,128)S(1)} %shard_map.125.h_ref.rest_0_), custom_call_target="tpu_custom_call" | custom-call | tf_op jit(solution)/shard_map/pallas_call | solution.py:22
  36.9 0.0 collective-permute-done.20.rest_2_
  36.9 0.0 collective-permute-done.25.rest_7_
  36.9 0.0 collective-permute-done.24.rest_6_
  36.9 0.0 collective-permute-done.21.rest_3_
  36.9 3.2 %shard_map.130 = (f32[32,128]{1,0:T(8,128)}, f32[16,32,128]{2,1,0:T(8,128)S(1)}, f32[16,32,128]{2,1,0:T(8,128)S(1)}, f32[1,32,128]{2,1,0:T(8,128)S(1)}, f32[1,32...) custom-call(f32[256,32]{1,0:T(8,128)S(1)} %get-tuple-element.35.mix_ref, ...), custom_call_target="tpu_custom_call" | custom-call | tf_op jit(solution)/shard_map/pallas_call | solution.py:22
  40.2 0.4 collective-permute-start.26
  40.6 3.5 %collective-permute-start.27 = (f32[1,32,128]{2,1,0:T(8,128)S(1)}, f32[1,32,128]{2,1,0:T(8,128)S(1)}, u32[]{:S(2)}, u32[]{:S(2)}) collective-permute-start(f32[1,32,128]{2,1,0:T(8,128)S(1)} %get-tuple-element.64), channel_id=1, source_target_pairs={{0,0},{8,16},{16,8},{24,24},{1,1},{9,17},{17,9},{25,25},{2,2},{10,... | collective-permute-start | bytes 49160 | tf_op jit(solution)/shard_map/ppermute | solution.py:98
  44.1 1.0 %collective-permute-start.28 = (f32[1,16,128]{2,1,0:T(8,128)S(1)}, f32[1,16,128]{2,1,0:T(8,128)S(1)}, u32[]{:S(2)}, u32[]{:S(2)}) collective-permute-start(f32[1,16,128]{2,1,0:T(8,128)S(1)} %get-tuple-element.65), channel_id=1, source_target_pairs={{0,4},{4,0},{1,5},{5,1},{2,6},{6,2},{3,7},{7,3},{8,12},{12,8},{9,1... | collective-permute-start | bytes 24584 | tf_op jit(solution)/shard_map/ppermute | solution.py:98
  45.1 0.0 collective-permute-start.29
  45.1 1.9 %collective-permute-start.30 = (f32[1,512]{1,0:T(1,128)S(1)}, f32[1,512]{1,0:T(1,128)S(1)}, u32[]{:S(2)}, u32[]{:S(2)}) collective-permute-start(f32[1,512]{1,0:T(1,128)S(1)} %get-tuple-element.67), channel_id=1, source_target_pairs={{0,0},{1,2},{2,1},{3,3},{4,4},{5,6},{6,5},{7,7},{8,8},{9,10},{10,9... | collective-permute-start | bytes 6152 | tf_op jit(solution)/shard_map/ppermute | solution.py:98
  47.0 0.4 shard_map.131.v_ref
  47.5 0.2 collective-permute-done.29.rest_3_
  47.7 1.8 %collective-permute-done.30.rest_4_ = f32[1,512]{1,0:T(1,128)S(1)} collective-permute-done((f32[1,512]{1,0:T(1,128)S(1)}, f32[1,512]{1,0:T(1,128)S(1)}, u32[]{:S(2)}, u32[]{:S(2)}) %collective-permute-start.30) | collective-permute-done | bytes 2080 | tf_op jit(solution)/shard_map/ppermute | solution.py:98
  49.4 1.2 %shard_map.132 = f32[16,32,128]{2,1,0:T(8,128)} custom-call(f32[16,32,128]{2,1,0:T(8,128)S(1)} %shard_map.131.v_ref, f32[2,32,128]{2,1,0:T(8,128)S(1)} %get-tuple-element.60.wx_ref, f32[2,16,128]{2,1,0:T(8,128)S(1)} %get-tuple-element.61.wy_ref, f32[16,32,128]{2,1,0:T(8,128)S(1)} %get-tuple-element.62.wz_ref, ...), custom_call_target="tpu_custom_call" | custom-call | tf_op jit(solution)/shard_map/pallas_call | solution.py:22
  (9 shorter events, 0.0 us)
Async XLA Ops:
  0.6 4.2 %collective-permute-start = (f32[32,128]{1,0:T(8,128)}, f32[32,128]{1,0:T(8,128)S(1)}, u32[]{:S(2)}, u32[]{:S(2)}) collective-permute-start(f32[32,128]{1,0:T(8,128)} %refs_3_.1), channel_id=1, source_target_pairs={{0,4},{4,0},{8,12},{12,8},{16,20},{20,16},{24,28},{28,24},{1,5},{5... | collective-permute-start | bytes 49160 | tf_op jit(solution)/shard_map/ppermute | solution.py:56
  1.9 3.9 %collective-permute-start.4 = (f32[32,128]{1,0:T(8,128)}, f32[32,128]{1,0:T(8,128)S(1)}, u32[]{:S(2)}, u32[]{:S(2)}) collective-permute-start(f32[32,128]{1,0:T(8,128)} %refs_3_.1), channel_id=1, source_target_pairs={{0,20},{4,16},{8,28},{12,24},{16,4},{20,0},{24,12},{28,8},{1,21},{... | collective-permute-start | bytes 49160 | tf_op jit(solution)/shard_map/ppermute | solution.py:56
  3.1 4.6 %collective-permute-start.3 = (f32[32,128]{1,0:T(8,128)}, f32[32,128]{1,0:T(8,128)S(1)}, u32[]{:S(2)}, u32[]{:S(2)}) collective-permute-start(f32[32,128]{1,0:T(8,128)} %refs_3_.1), channel_id=1, source_target_pairs={{0,16},{4,20},{8,24},{12,28},{16,0},{20,4},{24,8},{28,12},{1,17},{... | collective-permute-start | bytes 49160 | tf_op jit(solution)/shard_map/ppermute | solution.py:56
  3.3 8.0 %collective-permute-start.1 = (f32[32,128]{1,0:T(8,128)}, f32[32,128]{1,0:T(8,128)S(1)}, u32[]{:S(2)}, u32[]{:S(2)}) collective-permute-start(f32[32,128]{1,0:T(8,128)} %refs_3_.1), channel_id=1, source_target_pairs={{0,8},{4,12},{8,0},{12,4},{16,24},{20,28},{24,16},{28,20},{1,9},{5... | collective-permute-start | bytes 49160 | tf_op jit(solution)/shard_map/ppermute | solution.py:56
  4.9 6.5 %collective-permute-start.2 = (f32[32,128]{1,0:T(8,128)S(1)}, f32[32,128]{1,0:T(8,128)S(1)}, u32[]{:S(2)}, u32[]{:S(2)}) collective-permute-start(f32[32,128]{1,0:T(8,128)S(1)} %collective-permute-done.rest_1_), channel_id=1, source_target_pairs={{0,8},{4,12},{8,0},{12,4},{16,24},{20,28},{24,16},{28,20},{1,9},{5... | collective-permute-start | bytes 49160 | tf_op jit(solution)/shard_map/ppermute | solution.py:56
  5.8 5.6 %collective-permute-start.6 = (f32[32,128]{1,0:T(8,128)S(1)}, f32[32,128]{1,0:T(8,128)S(1)}, u32[]{:S(2)}, u32[]{:S(2)}) collective-permute-start(f32[32,128]{1,0:T(8,128)S(1)} %collective-permute-done.4.rest_5_), channel_id=1, source_target_pairs={{0,8},{4,12},{8,0},{12,4},{16,24},{20,28},{24,16},{28,20},{1,9},{5... | collective-permute-start | bytes 49160 | tf_op jit(solution)/shard_map/ppermute | solution.py:56
  7.7 3.6 %collective-permute-start.5 = (f32[32,128]{1,0:T(8,128)S(1)}, f32[32,128]{1,0:T(8,128)S(1)}, u32[]{:S(2)}, u32[]{:S(2)}) collective-permute-start(f32[32,128]{1,0:T(8,128)S(1)} %collective-permute-done.3.rest_4_), channel_id=1, source_target_pairs={{0,8},{4,12},{8,0},{12,4},{16,24},{20,28},{24,16},{28,20},{1,9},{5... | collective-permute-start | bytes 49160 | tf_op jit(solution)/shard_map/ppermute | solution.py:56
  11.6 3.6 %collective-permute-start.11 = (f32[32,128]{1,0:T(8,128)S(1)}, f32[32,128]{1,0:T(8,128)S(1)}, u32[]{:S(2)}, u32[]{:S(2)}) collective-permute-start(f32[32,128]{1,0:T(8,128)S(1)} %shard_map.123.h_ref.rest_0_), channel_id=1, source_target_pairs={{0,20},{4,16},{8,28},{12,24},{16,4},{20,0},{24,12},{28,8},{1,21},{... | collective-permute-start | bytes 49160 | tf_op jit(solution)/shard_map/ppermute | solution.py:56
  12.8 3.5 %collective-permute-start.10 = (f32[32,128]{1,0:T(8,128)S(1)}, f32[32,128]{1,0:T(8,128)S(1)}, u32[]{:S(2)}, u32[]{:S(2)}) collective-permute-start(f32[32,128]{1,0:T(8,128)S(1)} %shard_map.123.h_ref.rest_0_), channel_id=1, source_target_pairs={{0,16},{4,20},{8,24},{12,28},{16,0},{20,4},{24,8},{28,12},{1,17},{... | collective-permute-start | bytes 49160 | tf_op jit(solution)/shard_map/ppermute | solution.py:56
  14.1 2.8 %collective-permute-start.7 = (f32[32,128]{1,0:T(8,128)S(1)}, f32[32,128]{1,0:T(8,128)S(1)}, u32[]{:S(2)}, u32[]{:S(2)}) collective-permute-start(f32[32,128]{1,0:T(8,128)S(1)} %shard_map.123.h_ref.rest_0_), channel_id=1, source_target_pairs={{0,4},{4,0},{8,12},{12,8},{16,20},{20,16},{24,28},{28,24},{1,5},{5... | collective-permute-start | bytes 49160 | tf_op jit(solution)/shard_map/ppermute | solution.py:56
  14.3 4.1 %collective-permute-start.8 = (f32[32,128]{1,0:T(8,128)S(1)}, f32[32,128]{1,0:T(8,128)S(1)}, u32[]{:S(2)}, u32[]{:S(2)}) collective-permute-start(f32[32,128]{1,0:T(8,128)S(1)} %shard_map.123.h_ref.rest_0_), channel_id=1, source_target_pairs={{0,8},{4,12},{8,0},{12,4},{16,24},{20,28},{24,16},{28,20},{1,9},{5... | collective-permute-start | bytes 49160 | tf_op jit(solution)/shard_map/ppermute | solution.py:56
  15.2 3.5 %collective-permute-start.13 = (f32[32,128]{1,0:T(8,128)S(1)}, f32[32,128]{1,0:T(8,128)S(1)}, u32[]{:S(2)}, u32[]{:S(2)}) collective-permute-start(f32[32,128]{1,0:T(8,128)S(1)} %collective-permute-done.11.rest_5_), channel_id=1, source_target_pairs={{0,8},{4,12},{8,0},{12,4},{16,24},{20,28},{24,16},{28,20},{1,9},{5... | collective-permute-start | bytes 49160 | tf_op jit(solution)/shard_map/ppermute | solution.py:56
  16.3 2.5 %collective-permute-start.12 = (f32[32,128]{1,0:T(8,128)S(1)}, f32[32,128]{1,0:T(8,128)S(1)}, u32[]{:S(2)}, u32[]{:S(2)}) collective-permute-start(f32[32,128]{1,0:T(8,128)S(1)} %collective-permute-done.10.rest_4_), channel_id=1, source_target_pairs={{0,8},{4,12},{8,0},{12,4},{16,24},{20,28},{24,16},{28,20},{1,9},{5... | collective-permute-start | bytes 49160 | tf_op jit(solution)/shard_map/ppermute | solution.py:56
  16.8 6.9 %collective-permute-start.9 = (f32[32,128]{1,0:T(8,128)S(1)}, f32[32,128]{1,0:T(8,128)S(1)}, u32[]{:S(2)}, u32[]{:S(2)}) collective-permute-start(f32[32,128]{1,0:T(8,128)S(1)} %collective-permute-done.7.rest_1_), channel_id=1, source_target_pairs={{0,8},{4,12},{8,0},{12,4},{16,24},{20,28},{24,16},{28,20},{1,9},{5... | collective-permute-start | bytes 49160 | tf_op jit(solution)/shard_map/ppermute | solution.py:56
  18.4 12.7 %collective-permute-start.14 = (f32[2,32,128]{2,1,0:T(8,128)S(1)}, f32[2,32,128]{2,1,0:T(8,128)S(1)}, u32[]{:S(2)}, u32[]{:S(2)}) collective-permute-start(f32[2,32,128]{2,1,0:T(8,128)S(1)} %get-tuple-element.50), channel_id=1, source_target_pairs={{0,8},{8,0},{16,24},{24,16},{1,9},{9,1},{17,25},{25,17},{2,10},{10... | collective-permute-start | bytes 98312 | tf_op jit(solution)/shard_map/ppermute | solution.py:98
  18.4 11.5 %collective-permute-start.16 = (f32[2,16,128]{2,1,0:T(8,128)S(1)}, f32[2,16,128]{2,1,0:T(8,128)S(1)}, u32[]{:S(2)}, u32[]{:S(2)}) collective-permute-start(f32[2,16,128]{2,1,0:T(8,128)S(1)} %get-tuple-element.52), channel_id=1, source_target_pairs={{0,4},{4,0},{1,5},{5,1},{2,6},{6,2},{3,7},{7,3},{8,12},{12,8},{9,1... | collective-permute-start | bytes 49160 | tf_op jit(solution)/shard_map/ppermute | solution.py:98
  18.6 9.7 %collective-permute-start.17 = (f32[2,512]{1,0:T(2,128)S(1)}, f32[2,512]{1,0:T(2,128)S(1)}, u32[]{:S(2)}, u32[]{:S(2)}) collective-permute-start(f32[2,512]{1,0:T(2,128)S(1)} %get-tuple-element.53), channel_id=1, source_target_pairs={{0,1},{1,0},{2,3},{3,2},{4,5},{5,4},{6,7},{7,6},{8,9},{9,8},{10,11... | collective-permute-start | bytes 12296 | tf_op jit(solution)/shard_map/ppermute | solution.py:98
  18.8 9.6 %collective-permute-start.18 = (f32[2,512]{1,0:T(2,128)S(1)}, f32[2,512]{1,0:T(2,128)S(1)}, u32[]{:S(2)}, u32[]{:S(2)}) collective-permute-start(f32[2,512]{1,0:T(2,128)S(1)} %get-tuple-element.54), channel_id=1, source_target_pairs={{0,0},{1,2},{2,1},{3,3},{4,4},{5,6},{6,5},{7,7},{8,8},{9,10},{10,9... | collective-permute-start | bytes 12296 | tf_op jit(solution)/shard_map/ppermute | solution.py:98
  23.8 11.6 %collective-permute-start.15 = (f32[2,32,128]{2,1,0:T(8,128)S(1)}, f32[2,32,128]{2,1,0:T(8,128)S(1)}, u32[]{:S(2)}, u32[]{:S(2)}) collective-permute-start(f32[2,32,128]{2,1,0:T(8,128)S(1)} %get-tuple-element.51), channel_id=1, source_target_pairs={{0,0},{8,16},{16,8},{24,24},{1,1},{9,17},{17,9},{25,25},{2,2},{10,... | collective-permute-start | bytes 98312 | tf_op jit(solution)/shard_map/ppermute | solution.py:98
  28.3 3.6 %collective-permute-start.23 = (f32[32,128]{1,0:T(8,128)S(1)}, f32[32,128]{1,0:T(8,128)S(1)}, u32[]{:S(2)}, u32[]{:S(2)}) collective-permute-start(f32[32,128]{1,0:T(8,128)S(1)} %shard_map.125.h_ref.rest_0_), channel_id=1, source_target_pairs={{0,20},{4,16},{8,28},{12,24},{16,4},{20,0},{24,12},{28,8},{1,21},{... | collective-permute-start | bytes 49160 | tf_op jit(solution)/shard_map/ppermute | solution.py:56
  28.4 3.5 %collective-permute-start.22 = (f32[32,128]{1,0:T(8,128)S(1)}, f32[32,128]{1,0:T(8,128)S(1)}, u32[]{:S(2)}, u32[]{:S(2)}) collective-permute-start(f32[32,128]{1,0:T(8,128)S(1)} %shard_map.125.h_ref.rest_0_), channel_id=1, source_target_pairs={{0,16},{4,20},{8,24},{12,28},{16,0},{20,4},{24,8},{28,12},{1,17},{... | collective-permute-start | bytes 49160 | tf_op jit(solution)/shard_map/ppermute | solution.py:56
  29.9 3.0 %collective-permute-start.19 = (f32[32,128]{1,0:T(8,128)S(1)}, f32[32,128]{1,0:T(8,128)S(1)}, u32[]{:S(2)}, u32[]{:S(2)}) collective-permute-start(f32[32,128]{1,0:T(8,128)S(1)} %shard_map.125.h_ref.rest_0_), channel_id=1, source_target_pairs={{0,4},{4,0},{8,12},{12,8},{16,20},{20,16},{24,28},{28,24},{1,5},{5... | collective-permute-start | bytes 49160 | tf_op jit(solution)/shard_map/ppermute | solution.py:56
  31.1 5.8 %collective-permute-start.20 = (f32[32,128]{1,0:T(8,128)S(1)}, f32[32,128]{1,0:T(8,128)S(1)}, u32[]{:S(2)}, u32[]{:S(2)}) collective-permute-start(f32[32,128]{1,0:T(8,128)S(1)} %shard_map.125.h_ref.rest_0_), channel_id=1, source_target_pairs={{0,8},{4,12},{8,0},{12,4},{16,24},{20,28},{24,16},{28,20},{1,9},{5... | collective-permute-start | bytes 49160 | tf_op jit(solution)/shard_map/ppermute | solution.py:56
  31.9 5.0 %collective-permute-start.25 = (f32[32,128]{1,0:T(8,128)S(1)}, f32[32,128]{1,0:T(8,128)S(1)}, u32[]{:S(2)}, u32[]{:S(2)}) collective-permute-start(f32[32,128]{1,0:T(8,128)S(1)} %collective-permute-done.23.rest_5_), channel_id=1, source_target_pairs={{0,8},{4,12},{8,0},{12,4},{16,24},{20,28},{24,16},{28,20},{1,9},{5... | collective-permute-start | bytes 49160 | tf_op jit(solution)/shard_map/ppermute | solution.py:56
  31.9 5.0 %collective-permute-start.24 = (f32[32,128]{1,0:T(8,128)S(1)}, f32[32,128]{1,0:T(8,128)S(1)}, u32[]{:S(2)}, u32[]{:S(2)}) collective-permute-start(f32[32,128]{1,0:T(8,128)S(1)} %collective-permute-done.22.rest_4_), channel_id=1, source_target_pairs={{0,8},{4,12},{8,0},{12,4},{16,24},{20,28},{24,16},{28,20},{1,9},{5... | collective-permute-start | bytes 49160 | tf_op jit(solution)/shard_map/ppermute | solution.py:56
  32.8 4.1 %collective-permute-start.21 = (f32[32,128]{1,0:T(8,128)S(1)}, f32[32,128]{1,0:T(8,128)S(1)}, u32[]{:S(2)}, u32[]{:S(2)}) collective-permute-start(f32[32,128]{1,0:T(8,128)S(1)} %collective-permute-done.19.rest_1_), channel_id=1, source_target_pairs={{0,8},{4,12},{8,0},{12,4},{16,24},{20,28},{24,16},{28,20},{1,9},{5... | collective-permute-start | bytes 49160 | tf_op jit(solution)/shard_map/ppermute | solution.py:56
  40.2 9.3 %collective-permute-start.26 = (f32[1,32,128]{2,1,0:T(8,128)S(1)}, f32[1,32,128]{2,1,0:T(8,128)S(1)}, u32[]{:S(2)}, u32[]{:S(2)}) collective-permute-start(f32[1,32,128]{2,1,0:T(8,128)S(1)} %get-tuple-element.63), channel_id=1, source_target_pairs={{0,8},{8,0},{16,24},{24,16},{1,9},{9,1},{17,25},{25,17},{2,10},{10... | collective-permute-start | bytes 49160 | tf_op jit(solution)/shard_map/ppermute | solution.py:98
  40.6 8.8 %collective-permute-start.27 = (f32[1,32,128]{2,1,0:T(8,128)S(1)}, f32[1,32,128]{2,1,0:T(8,128)S(1)}, u32[]{:S(2)}, u32[]{:S(2)}) collective-permute-start(f32[1,32,128]{2,1,0:T(8,128)S(1)} %get-tuple-element.64), channel_id=1, source_target_pairs={{0,0},{8,16},{16,8},{24,24},{1,1},{9,17},{17,9},{25,25},{2,2},{10,... | collective-permute-start | bytes 49160 | tf_op jit(solution)/shard_map/ppermute | solution.py:98
  44.1 5.3 %collective-permute-start.28 = (f32[1,16,128]{2,1,0:T(8,128)S(1)}, f32[1,16,128]{2,1,0:T(8,128)S(1)}, u32[]{:S(2)}, u32[]{:S(2)}) collective-permute-start(f32[1,16,128]{2,1,0:T(8,128)S(1)} %get-tuple-element.65), channel_id=1, source_target_pairs={{0,4},{4,0},{1,5},{5,1},{2,6},{6,2},{3,7},{7,3},{8,12},{12,8},{9,1... | collective-permute-start | bytes 24584 | tf_op jit(solution)/shard_map/ppermute | solution.py:98
  45.1 2.5 %collective-permute-start.29 = (f32[1,512]{1,0:T(1,128)S(1)}, f32[1,512]{1,0:T(1,128)S(1)}, u32[]{:S(2)}, u32[]{:S(2)}) collective-permute-start(f32[1,512]{1,0:T(1,128)S(1)} %get-tuple-element.66), channel_id=1, source_target_pairs={{0,1},{1,0},{2,3},{3,2},{4,5},{5,4},{6,7},{7,6},{8,9},{9,8},{10,11... | collective-permute-start | bytes 6152 | tf_op jit(solution)/shard_map/ppermute | solution.py:98
  45.1 4.3 %collective-permute-start.30 = (f32[1,512]{1,0:T(1,128)S(1)}, f32[1,512]{1,0:T(1,128)S(1)}, u32[]{:S(2)}, u32[]{:S(2)}) collective-permute-start(f32[1,512]{1,0:T(1,128)S(1)} %get-tuple-element.67), channel_id=1, source_target_pairs={{0,0},{1,2},{2,1},{3,3},{4,4},{5,6},{6,5},{7,7},{8,8},{9,10},{10,9... | collective-permute-start | bytes 6152 | tf_op jit(solution)/shard_map/ppermute | solution.py:98
where the time goes:
time: 50.8 us; the launch traced here: 50.6 us
  starting transfers between devices  33.6 us (66%)
  Pallas kernels  12.9 us (25%)
  waiting for transfers between devices  3.32 us (7%)
  between operations  0.81 us (2%)
    ppermute x21, starting transfers between devices, swap(): return lax.ppermute(x, GROUP, [(i, i ^ k) for i in range(n)])  17.7 us
    ppermute x10, starting transfers between devices, exchange(): out.append(lax.ppermute(face, axis, pair_lists(lax.axis_size(axis))[r]))  15.9 us
    pallas_call x11, Pallas kernels, call(): pl.pallas_call(body, out_shape=out_shape, in_specs=[pl.BlockSpec(memory_s...  12.9 us
    ppermute x10, waiting for transfers between devices, exchange(): out.append(lax.ppermute(face, axis, pair_lists(lax.axis_size(axis))[r]))  1.99 us
    ppermute x21, waiting for transfers between devices, swap(): return lax.ppermute(x, GROUP, [(i, i ^ k) for i in range(n)])  1.33 us
  transfers between devices with their start and end apart: 31, of which 4 were waited for; matrix products, arithmetic and copies ran while one was open for 0% of the time, Pallas kernels for 16%

commit v1 on v0

v1 whole, which is shorter than its diff:
```python
import functools

import jax
import jax.numpy as jnp
from jax import lax
from jax.experimental import pallas as pl
from jax.experimental.pallas import tpu as pltpu
from jax.sharding import PartitionSpec as P


SWEEPS = 3
AXES = ("gx", "gy", "gz")
GROUP = ("gx", "gy")
F32 = jnp.float32
BF16 = jnp.bfloat16
HIGH = lax.Precision.HIGHEST


def call(body, out_shape, *args, scratch=(), hbm=0):
    vmem = pl.BlockSpec(memory_space=pltpu.VMEM)
    args = [pltpu.with_memory_space_constraint(x, pltpu.HBM) for x in args[:hbm]] + list(args[hbm:])
    return pl.pallas_call(
        body,
        out_shape=out_shape,
        in_specs=[pl.BlockSpec(memory_space=pltpu.HBM)] * hbm + [vmem] * (len(args) - hbm),
        scratch_shapes=scratch,
        compiler_params=pltpu.CompilerParams(vmem_limit_bytes=48 << 20),
    )(*args)


def sds(shape, dtype=F32):
    return jax.ShapeDtypeStruct(shape, dtype)


def iota(shape, dim):
    return lax.broadcasted_iota(jnp.int32, shape, dim)


def dot(a, b, ca, cb, precision=None):
    return lax.dot_general(
        a, b, (((ca,), (cb,)), ((), ())), precision=precision, preferred_element_type=F32
    )


def group_size():
    return lax.axis_size("gx") * lax.axis_size("gy")


def by_pairs():
    return lax.axis_size("gx") == 4 and lax.axis_size("gy") == 2


def swap(x, k):
    n = group_size()
    return lax.ppermute(x, GROUP, [(i, i ^ k) for i in range(n)])


def meet(direct, own):
    low = lax.axis_size("gy")
    slots = {k: swap(x, k) for k, x in direct.items()}
    slots[low] = swap(own, low)
    for k in direct:
        slots[k | low] = swap(slots[k], low)
    return slots


def pair_lists(count):
    first = [(i, i ^ 1 if (i ^ 1) < count else i) for i in range(count)]
    second = []
    for i in range(count):
        j = i + 1 if i % 2 else i - 1
        second.append((i, j if 0 <= j < count else i))
    return first, second


def rounds_of(axis):
    count = lax.axis_size(axis)
    return 0 if count == 1 else 1 if count == 2 else 2


def face_specs(shape, lead):
    nx, ny, nz = shape
    full = {"gx": (lead, ny, nz), "gy": (lead, nx, nz), "gz": (lead, nx * ny)}
    return [(axis, r, full[axis]) for axis in AXES for r in range(rounds_of(axis))]


def exchange(faces, specs):
    out = []
    for face, (axis, r, _) in zip(faces, specs):
        out.append(lax.ppermute(face, axis, pair_lists(lax.axis_size(axis))[r]))
    return out


def face_of(t, axis, r):
    nx, ny, nz = t.shape
    even = lax.axis_index(axis) % 2 == 0
    high = even if r == 0 else jnp.logical_not(even)
    if axis == "gx":
        return jnp.where(high, t[nx - 1], t[0])
    if axis == "gy":
        return jnp.where(high, t[:, ny - 1, :], t[:, 0, :])
    lane = jnp.where(high, nz - 1, 0)
    pick = (iota((8, nz), 1) == lane).astype(F32)
    return dot(pick, t.reshape(nx * ny, nz), 1, 1, HIGH)[0:1, :]


def write_faces(refs, specs, fields):
    for ref, (axis, r, _) in zip(refs, specs):
        for j, t in enumerate(fields):
            face = face_of(t, axis, r)
            if axis == "gz":
                ref[j : j + 1, :] = face
            else:
                ref[j] = face


def read_faces(refs, specs, j):
    got = {axis: [] for axis in AXES}
    for ref, (axis, r, _) in zip(refs, specs):
        got[axis].append(ref[j : j + 1, :] if axis == "gz" else ref[j])
    return got


def ghosts_of(axis, faces, like):
    zero = jnp.zeros(like, F32)
    if not faces:
        return zero, zero
    index, count = lax.axis_index(axis), lax.axis_size(axis)
    even = index % 2 == 0
    second = faces[1] if len(faces) > 1 else zero
    low = jnp.where(even, second, faces[0])
    high = jnp.where(even, faces[0], second)
    return jnp.where(index > 0, low, zero), jnp.where(index < count - 1, high, zero)


def embed_z(pair, shape):
    nx, ny, nz = shape
    low, high = pair
    rows = jnp.concatenate([low, high, jnp.zeros((6, nx * ny), F32)], axis=0)
    lane = jnp.where(iota((8, nz), 0) == 0, 0, nz - 1)
    pick = ((iota((8, nz), 1) == lane) & (iota((8, nz), 0) < 2)).astype(F32)
    return dot(rows, pick, 0, 0, HIGH).reshape(shape)


def interior(t, c):
    shape = t.shape
    _, ny, nz = shape
    gain = jnp.zeros(shape, F32)
    weight = jnp.zeros(shape, F32)
    wx = 0.5 * (c[:-1] + c[1:])
    none = jnp.zeros((1, ny, nz), F32)
    w_low = jnp.concatenate([none, wx], axis=0)
    w_high = jnp.concatenate([wx, none], axis=0)
    t_low = jnp.concatenate([none, t[:-1]], axis=0)
    t_high = jnp.concatenate([t[1:], none], axis=0)
    gain = gain + w_low * t_low + w_high * t_high
    weight = weight + w_low + w_high
    for dim, n in ((1, ny), (2, nz)):
        at = iota(shape, dim)
        for shift, edge in ((1, 0), (n - 1, n - 1)):
            w = jnp.where(at == edge, 0.0, 0.5 * (c + pltpu.roll(c, shift, dim)))
            gain = gain + w * pltpu.roll(t, shift, dim)
            weight = weight + w
    return gain, weight


def shards(
    initial_hydraulic_head,
    well_discharge,
    local_facet_coupling,
    diagonal_capacity,
    crossing_permeability,
    crossing_partner_number,
    liquid_thermal_state,
    transfer_factor,
    host_voxel_number,
    stone_thermal_state,
    matrix_diffusivity,
):
    nb, links = crossing_partner_number.shape
    tri = initial_hydraulic_head.shape[1]
    shape = stone_thermal_state.shape
    nx, ny, nz = shape
    rows_n = nx * ny
    n = group_size()
    low = lax.axis_size("gy")
    pairs = by_pairs() and 4 * nb == tri
    specs2 = face_specs(shape, 2)
    specs1 = face_specs(shape, 1)
    xy = [i for i, spec in enumerate(specs2) if spec[0] != "gz"]
    zs = [i for i, spec in enumerate(specs2) if spec[0] == "gz"]
    blk = sds((nb, tri))
    slab = sds(shape)
    small = -(-2 * links // 8) * 8

    def load(copies):
        copies = [pltpu.make_async_copy(src, dst, sem) for src, dst, sem in copies]
        for copy in copies:
            copy.start()
        return copies

    def inner_of(a_ref, h):
        h = h.astype(BF16)
        return jnp.concatenate([dot(h[b : b + 1, :], a_ref[b], 1, 1) for b in range(nb)], axis=0)

    def mix_of(ids, perm):
        at = iota((n * nb, ids.shape[1]), 0)
        mix = jnp.zeros(at.shape, F32)
        for k in range(links):
            mix = mix + jnp.where(at == ids[k : k + 1, :], perm[k : k + 1, :], 0.0)
        return mix

    def pre(ids_hbm, perm_hbm, diag_hbm, h_hbm, w_hbm, a_hbm, send_ref, w_ref, a_ref, ids_ref, perm_ref, den_ref, h_ref, sems):
        pieces = ((ids_hbm, ids_ref), (perm_hbm, perm_ref), (diag_hbm, den_ref), (h_hbm, h_ref), (w_hbm, w_ref), (a_hbm, a_ref))
        copies = load([(src, dst, sems.at[i]) for i, (src, dst) in enumerate(pieces)])
        send_ref[3 * nb :, :] = jnp.zeros((small, tri), F32)
        for copy in copies[:5]:
            copy.wait()
        perm = perm_ref[...]
        send_ref[3 * nb : 3 * nb + links, :nb] = ids_ref[...].astype(F32)
        send_ref[3 * nb + links : 3 * nb + 2 * links, :nb] = perm
        rows = jnp.concatenate([perm, jnp.zeros((-links % 8, nb), F32)], axis=0)
        send_ref[2 * nb : 3 * nb, :] = den_ref[...] + dot(rows, jnp.ones((rows.shape[0], tri), F32), 0, 0, HIGH)
        h = h_ref[...]
        send_ref[:nb, :] = h
        copies[5].wait()
        send_ref[nb : 2 * nb, :] = w_ref[...] + inner_of(a_ref, h)

    def rock(*refs):
        nf = len(specs2)
        hbm, kept, faces, sems = refs[:5], refs[5:10], refs[10 : 10 + nf], refs[-1]
        copies = load([(src, dst, sems.at[i]) for i, (src, dst) in enumerate(zip(hbm, kept))])
        for copy in copies:
            copy.wait()
        write_faces(faces, specs2, (kept[0][...], kept[1][...]))

    def both(w_ref, a_ref, *rest):
        slots, rest = rest[:n], rest[n:]
        faces, (h_ref, mix_ref, *sends) = rest[: len(xy)], rest[len(xy) :]
        me = lax.axis_index("gx") * low + lax.axis_index("gy")
        heads = jnp.concatenate([s[:nb, :] for s in slots], axis=0)
        per = tri // nb
        first = []
        for g in range(0, n, per):
            table = slots[g][3 * nb :, :]
            for i in range(1, per):
                table = table + pltpu.roll(slots[g + i][3 * nb :, :], i * nb, 1)
            ids = table[:links, :].astype(jnp.int32) ^ (me * nb)
            mix = mix_of(ids, table[links : 2 * links, :])
            if g == 0:
                mix_ref[...] = mix
            across = dot(mix, heads, 0, 0, HIGH)
            for i in range(per):
                s = slots[g + i]
                first.append((s[nb : 2 * nb, :] + across[i * nb : (i + 1) * nb, :]) / s[2 * nb : 3 * nb, :])
        inner = inner_of(a_ref, first[0])
        across = dot(mix_ref[...], jnp.concatenate(first, axis=0), 0, 0, HIGH)[:nb, :]
        h = (w_ref[...] + inner + across) / slots[0][2 * nb : 3 * nb, :]
        h_ref[...] = h
        for send, face in zip(sends, faces):
            send[:nb, :] = h
            half = face.shape[1]
            send[nb : nb + half, :] = face[0]
            send[nb + half : nb + 2 * half, :] = face[1]

    def inner_body(a_ref, h_ref, o_ref):
        o_ref[...] = inner_of(a_ref, h_ref[...])

    def sweep(w_ref, den_ref, mix_ref, inner_ref, heads):
        across = dot(mix_ref[...], heads, 0, 0, HIGH)[:nb, :]
        return (w_ref[...] + inner_ref[...] + across) / den_ref[...]

    def gather(first, t_ref, hv_ref, liq_ref, tf_ref, q_ref, hot_ref):
        t = t_ref[...].reshape(rows_n, nz)
        hi = t.astype(BF16)
        lo = (t - hi.astype(F32)).astype(BF16)
        parts = jnp.concatenate([hi, lo], axis=1)
        hv = hv_ref[...]
        step = 4
        half = hot_ref.shape[1] // tri
        for b in range(0, half, step):
            cell = jnp.concatenate([hv[first + i : first + i + 1, :] for i in range(b, b + step)], axis=1)
            width = step * tri
            hot = (iota((rows_n, width), 0) == cell // nz).astype(F32).astype(BF16)
            hot_ref[:, b * tri : b * tri + width] = hot
            rows = dot(parts, hot, 0, 0)
            rows = rows[:nz] + rows[nz:]
            value = jnp.sum(jnp.where(iota((nz, width), 0) == cell % nz, rows, 0.0), axis=0, keepdims=True)
            for i in range(step):
                q_ref[b + i : b + i + 1, :] = value[:, i * tri : (i + 1) * tri]
        own = slice(first, first + half)
        q_ref[...] = tf_ref[own, :] * (liq_ref[own, :] - q_ref[...])

    def base(t_ref, c_ref, *rest):
        got, (u_ref, keep_ref, wz_ref) = rest[: len(zs)], rest[len(zs) :]
        specs = [specs2[i] for i in zs]
        t, c = t_ref[...], c_ref[...]
        tz = ghosts_of("gz", read_faces(got, specs, 0)["gz"], (1, rows_n))
        cz = ghosts_of("gz", read_faces(got, specs, 1)["gz"], (1, rows_n))
        gain, weight = interior(t, c)
        at = iota(shape, 2)
        wz = jnp.where((at == 0) | (at == nz - 1), 0.5 * (c + embed_z(cz, shape)), 0.0)
        keep = 1.0 - weight - wz
        wz_ref[...] = wz
        keep_ref[...] = keep
        u_ref[...] = gain + t * keep + wz * embed_z(tz, shape)

    def add_sides(u_ref, t_ref, wx_ref, wy_ref, gx, gy):
        for i, at in enumerate((0, nx - 1)):
            u_ref[at] = u_ref[at] + wx_ref[i] * (gx[i] - t_ref[at])
        for i, at in enumerate((0, ny - 1)):
            u_ref[:, at, :] = u_ref[:, at, :] + wy_ref[i] * (gy[i] - t_ref[:, at, :])

    def heat(get_sides, get_heads, ns, *refs):
        mix_ref, den_ref, w_ref, inner_ref, q1_ref, q2_ref, hv_ref, hot1_ref, hot2_ref, u_ref, t0_ref, c_ref = refs[:12]
        got, rest = refs[12 : 12 + ns], refs[12 + ns :]
        h_ref, f_ref, t_ref, wx_ref, wy_ref, *faces = rest[:-1]
        pick_ref = rest[-1]
        h = sweep(w_ref, den_ref, mix_ref, inner_ref, get_heads(got))
        h_ref[...] = h
        q = jnp.concatenate([q1_ref[...], q2_ref[...]], axis=0)
        flux = q * jnp.sqrt(1.0 + h * h)
        hi = flux.astype(BF16).astype(F32)
        lo = flux - hi
        lane = hv_ref[...] % nz
        for b in range(nb):
            mask = iota((nz, tri), 0) == lane[b : b + 1, :]
            pick_ref[:nz, b * tri : (b + 1) * tri] = jnp.where(mask, hi[b : b + 1, :], 0.0).astype(BF16)
            pick_ref[nz:, b * tri : (b + 1) * tri] = jnp.where(mask, lo[b : b + 1, :], 0.0).astype(BF16)
        half = hot1_ref.shape[1]
        parts = dot(hot1_ref[...], pick_ref[:, :half], 1, 1) + dot(hot2_ref[...], pick_ref[:, half:], 1, 1)
        f = (parts[:, :nz] + parts[:, nz:]).reshape(shape)
        f_ref[...] = f
        t_ref[...] = u_ref[...] + f
        tx, ty = get_sides(got, 0)
        cx, cy = get_sides(got, 1)
        for i, at in enumerate((0, nx - 1)):
            wx_ref[i] = 0.5 * (c_ref[at] + cx[i])
        for i, at in enumerate((0, ny - 1)):
            wy_ref[i] = 0.5 * (c_ref[:, at, :] + cy[i])
        add_sides(t_ref, t0_ref, wx_ref, wy_ref, tx, ty)
        write_faces(faces, specs1, (t_ref[...],))

    def middle(t_ref, f_ref, c_ref, keep_ref, v_ref):
        t = t_ref[...]
        gain, _ = interior(t, c_ref[...])
        v_ref[...] = f_ref[...] + t * keep_ref[...] + gain

    def last(v_ref, t_ref, wx_ref, wy_ref, wz_ref, *rest):
        got, o_ref = rest[:-1], rest[-1]
        faces = read_faces(got, specs1, 0)
        o_ref[...] = v_ref[...] + wz_ref[...] * embed_z(ghosts_of("gz", faces["gz"], (1, rows_n)), shape)
        gx = ghosts_of("gx", faces["gx"], (ny, nz))
        gy = ghosts_of("gy", faces["gy"], (nx, nz))
        add_sides(o_ref, t_ref, wx_ref, wy_ref, gx, gy)

    send, w, a = call(
        pre,
        (sds((3 * nb + small, tri)), blk, sds(local_facet_coupling.shape, BF16)),
        crossing_partner_number.T,
        crossing_permeability.T,
        diagonal_capacity,
        initial_hydraulic_head,
        well_discharge,
        local_facet_coupling,
        scratch=[pltpu.VMEM((links, nb), jnp.int32), pltpu.VMEM((links, nb), F32)]
        + [pltpu.VMEM((nb, tri), F32)] * 2
        + [pltpu.SemaphoreType.DMA((6,))],
        hbm=6,
    )
    if pairs:
        slots = meet({k: send for k in range(n - 1, 0, -1) if not k & low}, send)
    t, c, hv, liq, tf, *faces = call(
        rock,
        [slab, slab, sds((nb, tri), jnp.int32), blk, blk] + [sds(s) for _, _, s in specs2],
        stone_thermal_state,
        matrix_diffusivity,
        host_voxel_number,
        liquid_thermal_state,
        transfer_factor,
        scratch=[pltpu.SemaphoreType.DMA((5,))],
        hbm=5,
    )
    got_z = exchange([faces[i] for i in zs], [specs2[i] for i in zs])
    if pairs:
        y_at, xa_at, xb_at = 1, low, 2 * low
        order = {"gx": (xa_at, xb_at), "gy": (y_at,)}
        rides = [order[specs2[i][0]][specs2[i][1]] for i in xy]
        h, mix, *sends = call(
            both,
            [blk, sds((n * nb, tri))] + [sds((nb + 2 * specs2[i][2][1], tri)) for i in xy],
            w,
            a,
            send,
            *[slots[k] for k in range(1, n)],
            *[faces[i] for i in xy],
        )
        ride = dict(zip(rides, sends))
        slots = meet({k: ride.get(k, h) for k in range(n - 1, 0, -1) if not k & low}, ride[low])
        den = send[2 * nb : 3 * nb]
        got = [h] + [slots[k] for k in range(1, n)]

        def get_heads(refs):
            return jnp.concatenate([r[:nb, :] for r in refs], axis=0)

        def get_sides(refs, j):
            x_rows, y_rows = slice(nb + j * ny, nb + (j + 1) * ny), slice(nb + j * nx, nb + (j + 1) * nx)
            gx = ghosts_of("gx", [refs[xa_at][x_rows, :], refs[xb_at | low][x_rows, :]], (ny, nz))
            return gx, ghosts_of("gy", [refs[y_at][y_rows, :]], (nx, nz))
    else:
        den = send[2 * nb : 3 * nb]
        h = initial_hydraulic_head
        ids = jnp.zeros((small, tri), jnp.int32).at[:links, :nb].set(crossing_partner_number.T)
        perm = send[3 * nb + links : 3 * nb + 2 * links]

        def mix_body(ids_ref, perm_ref, mix_ref):
            mix_ref[...] = mix_of(ids_ref[...], perm_ref[...])

        def sweep_body(w_ref, den_ref, mix_ref, inner_ref, heads_ref, h_ref):
            h_ref[...] = sweep(w_ref, den_ref, mix_ref, inner_ref, heads_ref[...])

        mix = call(mix_body, sds((n * nb, tri)), ids[:links], perm)
        for _ in range(SWEEPS - 1):
            heads = lax.all_gather(h, GROUP, axis=0, tiled=True)
            inner = call(inner_body, blk, a, h)
            h = call(sweep_body, blk, w, den, mix, inner, heads)
        got = [lax.all_gather(h, GROUP, axis=0, tiled=True)]
        got += exchange([faces[i] for i in xy], [specs2[i] for i in xy])

        def get_heads(refs):
            return refs[0][...]

        def get_sides(refs, j):
            sides = read_faces(refs[1:], [specs2[i] for i in xy], j)
            return ghosts_of("gx", sides["gx"], (ny, nz)), ghosts_of("gy", sides["gy"], (nx, nz))

    inner = call(inner_body, blk, a, h)
    half = nb // 2
    parts = [
        call(functools.partial(gather, i * half), (sds((half, tri)), sds((rows_n, half * tri), BF16)), t, hv, liq, tf)
        for i in range(2)
    ]
    (q1, hot1), (q2, hot2) = parts
    u, keep, wz = call(base, (slab, slab, slab), t, c, *got_z)
    h, f, t1, wx, wy, *faces = call(
        functools.partial(heat, get_sides, get_heads, len(got)),
        [blk, slab, slab, sds((2, ny, nz)), sds((2, nx, nz))] + [sds(s) for _, _, s in specs1],
        mix,
        den,
        w,
        inner,
        q1,
        q2,
        hv,
        hot1,
        hot2,
        u,
        t,
        c,
        *got,
        scratch=[pltpu.VMEM((2 * nz, nb * tri), BF16)],
    )
    got = exchange(faces, specs1)
    v = call(middle, slab, t1, f, c, keep)
    out = call(last, slab, v, t1, wx, wy, wz, *got)
    return (h, out)


def solution(mesh):
    block = P(AXES, None)
    rock = P(*AXES)
    in_specs = (block, block, P(AXES, None, None)) + (block,) * 6 + (rock, rock)

    return jax.shard_map(shards, mesh=mesh, in_specs=in_specs, out_specs=(block, rock), check_vma=False)
```

time: 50.8 us -> 46.4 us (0.913)
  the two profiles are of different devices: /device:TPU:9 before, /device:TPU:12 now
where the time goes in v1:
time: 46.4 us; the launch traced here: 46.2 us
  starting transfers between devices  15.7 us (34%)
  waiting for transfers between devices  15.6 us (34%)
  Pallas kernels  14.1 us (30%)
  between operations  0.8 us (2%)
    pallas_call x10, Pallas kernels, call(): pl.pallas_call(body, out_shape=out_shape, in_specs=[pl.BlockSpec(memory_s...  14.1 us
    ppermute x14, waiting for transfers between devices, swap(): return lax.ppermute(x, GROUP, [(i, i ^ k) for i in range(n)])  10.4 us
    ppermute x7, starting transfers between devices, exchange(): out.append(lax.ppermute(face, axis, pair_lists(lax.axis_size(axis))[r]))  10.1 us
    ppermute x14, starting transfers between devices, swap(): return lax.ppermute(x, GROUP, [(i, i ^ k) for i in range(n)])  5.61 us
    ppermute x7, waiting for transfers between devices, exchange(): out.append(lax.ppermute(face, axis, pair_lists(lax.axis_size(axis))[r]))  5.2 us
  transfers between devices with their start and end apart: 21, of which 8 were waited for; matrix products, arithmetic and copies ran while one was open for 0% of the time, Pallas kernels for 14%

profile of v1, /device:TPU:12, one launch (start us, length us, event | category | flops | bytes accessed | tf_op | source)
XLA Modules:
  0.0 46.2 jit_solution(18121394420339482057)
XLA Ops:
  0.6 2.0 %shard_map.122 = (f32[104,128]{1,0:T(8,128)S(1)}, f32[32,128]{1,0:T(8,128)S(1)}, bf16[32,128,128]{2,1,0:T(8,128)(2,1)S(1)}) custom-call(s32[4,32]{1,0:T(4,128)} %bitcast.2, f32[4,32]{1,0:T(4,128)} %bitcast.3, f32[32,128]{1,0:T(8,128)} %diag_hbm.1, f32[32,128]{1,0:T(8,128)} %h_hbm.1, f32[32,128]{1,0:T(8,128)} %w_hbm.1, bf16[32,128,128]{2,1,0:T(8,128)(2,1)} %a_hbm.1), custom_call_target="tpu_custom_call" | custom-call | tf_op jit(solution)/shard_map/pallas_call | solution.py:22
  2.7 1.5 %collective-permute-start.4 = (f32[104,128]{1,0:T(8,128)S(1)}, f32[104,128]{1,0:T(8,128)S(1)}, u32[]{:S(2)}, u32[]{:S(2)}) collective-permute-start(f32[104,128]{1,0:T(8,128)S(1)} %get-tuple-element.39.rest_0_), channel_id=1, source_target_pairs={{0,20},{4,16},{8,28},{12,24},{16,4},{20,0},{24,12},{28,8},{1,21},{... | collective-permute-start | bytes 159752 | tf_op jit(solution)/shard_map/ppermute | solution.py:55
  4.2 1.5 %collective-permute-start.3 = (f32[104,128]{1,0:T(8,128)S(1)}, f32[104,128]{1,0:T(8,128)S(1)}, u32[]{:S(2)}, u32[]{:S(2)}) collective-permute-start(f32[104,128]{1,0:T(8,128)S(1)} %get-tuple-element.39.rest_0_), channel_id=1, source_target_pairs={{0,16},{4,20},{8,24},{12,28},{16,0},{20,4},{24,8},{28,12},{1,17},{... | collective-permute-start | bytes 159752 | tf_op jit(solution)/shard_map/ppermute | solution.py:55
  5.7 0.5 %collective-permute-start = (f32[104,128]{1,0:T(8,128)S(1)}, f32[104,128]{1,0:T(8,128)S(1)}, u32[]{:S(2)}, u32[]{:S(2)}) collective-permute-start(f32[104,128]{1,0:T(8,128)S(1)} %get-tuple-element.39.rest_0_), channel_id=1, source_target_pairs={{0,4},{4,0},{8,12},{12,8},{16,20},{20,16},{24,28},{28,24},{1,5},{5... | collective-permute-start | bytes 159752 | tf_op jit(solution)/shard_map/ppermute | solution.py:55
  6.2 0.0 collective-permute-start.1
  6.2 1.8 %collective-permute-done.4.rest_5_ = f32[104,128]{1,0:T(8,128)S(1)} collective-permute-done((f32[104,128]{1,0:T(8,128)S(1)}, f32[104,128]{1,0:T(8,128)S(1)}, u32[]{:S(2)}, u32[]{:S(2)}) %collective-permute-start.4) | collective-permute-done | bytes 53280 | tf_op jit(solution)/shard_map/ppermute | solution.py:55
  8.0 0.0 collective-permute-start.6
  8.0 0.4 collective-permute-done.3.rest_4_
  8.4 0.1 collective-permute-start.5
  8.5 1.3 %collective-permute-done.rest_1_ = f32[104,128]{1,0:T(8,128)S(1)} collective-permute-done((f32[104,128]{1,0:T(8,128)S(1)}, f32[104,128]{1,0:T(8,128)S(1)}, u32[]{:S(2)}, u32[]{:S(2)}) %collective-permute-start) | collective-permute-done | bytes 53280 | tf_op jit(solution)/shard_map/ppermute | solution.py:55
  9.8 0.0 collective-permute-start.2
  9.8 2.0 %shard_map.123 = (f32[16,32,128]{2,1,0:T(8,128)S(1)}, f32[16,32,128]{2,1,0:T(8,128)S(1)}, s32[32,128]{1,0:T(8,128)S(1)}, f32[32,128]{1,0:T(8,128)S(1)}, f32[32,1...) custom-call(f32[16,32,128]{2,1,0:T(8,128)} %refs_0_.1, ...), custom_call_target="tpu_custom_call" | custom-call | tf_op jit(solution)/shard_map/pallas_call | solution.py:22
  11.8 0.0 collective-permute-done.1.rest_2_
  11.9 0.0 collective-permute-done.6.rest_7_
  11.9 0.0 collective-permute-done.5.rest_6_
  11.9 0.0 collective-permute-done.2.rest_3_
  11.9 1.2 %shard_map.124 = (f32[32,128]{1,0:T(8,128)S(1)}, f32[256,128]{1,0:T(8,128)S(1)}, f32[96,128]{1,0:T(8,128)S(1)}, f32[96,128]{1,0:T(8,128)S(1)}, f32[64,128]{1,0:T(8,128)S(1)}) custom-call(f32[32,128]{1,0:T(8,128)S(1)} %get-tuple-element.37.w_ref.refs_2_, bf16[32,128,128]{2,1,0:T(8,128)(2,1)S(1)} %get-tuple-element.38.a_ref, ...), custom_call_target="tpu_custom_call" | custom-call | tf_op jit(solution)/shard_map/pallas_call | solution.py:22
  13.1 0.6 %collective-permute-start.12 = (f32[96,128]{1,0:T(8,128)S(1)}, f32[96,128]{1,0:T(8,128)S(1)}, u32[]{:S(2)}, u32[]{:S(2)}) collective-permute-start(f32[96,128]{1,0:T(8,128)S(1)} %get-tuple-element.59), channel_id=1, source_target_pairs={{0,16},{4,20},{8,24},{12,28},{16,0},{20,4},{24,8},{28,12},{1,17},{... | collective-permute-start | bytes 147464 | tf_op jit(solution)/shard_map/ppermute | solution.py:55
  13.7 0.6 %collective-permute-start.9 = (f32[64,128]{1,0:T(8,128)S(1)}, f32[64,128]{1,0:T(8,128)S(1)}, u32[]{:S(2)}, u32[]{:S(2)}) collective-permute-start(f32[64,128]{1,0:T(8,128)S(1)} %get-tuple-element.57), channel_id=1, source_target_pairs={{0,4},{4,0},{8,12},{12,8},{16,20},{20,16},{24,28},{28,24},{1,5},{5... | collective-permute-start | bytes 98312 | tf_op jit(solution)/shard_map/ppermute | solution.py:55
  14.3 0.0 collective-permute-start.10
  14.4 3.0 %collective-permute-done.12.refs_16_ = f32[96,128]{1,0:T(8,128)S(1)} collective-permute-done((f32[96,128]{1,0:T(8,128)S(1)}, f32[96,128]{1,0:T(8,128)S(1)}, u32[]{:S(2)}, u32[]{:S(2)}) %collective-permute-start.12) | collective-permute-done | bytes 49184 | tf_op jit(solution)/shard_map/ppermute | solution.py:55
  17.4 0.0 collective-permute-start.14
  17.4 0.5 %collective-permute-start.13 = (f32[32,128]{1,0:T(8,128)S(1)}, f32[32,128]{1,0:T(8,128)S(1)}, u32[]{:S(2)}, u32[]{:S(2)}) collective-permute-start(f32[32,128]{1,0:T(8,128)S(1)} %get-tuple-element.44.h_ref.refs_12_), channel_id=1, source_target_pairs={{0,20},{4,16},{8,28},{12,24},{16,4},{20,0},{24,12},{28,8},{1,21},{... | collective-permute-start | bytes 49160 | tf_op jit(solution)/shard_map/ppermute | solution.py:55
  17.9 0.0 collective-permute-done.9.refs_13_
  17.9 0.2 collective-permute-start.11
  18.1 3.9 %collective-permute-done.13.refs_17_ = f32[32,128]{1,0:T(8,128)S(1)} collective-permute-done((f32[32,128]{1,0:T(8,128)S(1)}, f32[32,128]{1,0:T(8,128)S(1)}, u32[]{:S(2)}, u32[]{:S(2)}) %collective-permute-start.13) | collective-permute-done | bytes 16416 | tf_op jit(solution)/shard_map/ppermute | solution.py:55
  22.0 0.0 collective-permute-start.15
  22.0 0.4 collective-permute-start.7
  22.5 3.2 %collective-permute-done.7.rest_0_ = f32[2,512]{1,0:T(2,128)S(1)} collective-permute-done((f32[2,512]{1,0:T(2,128)S(1)}, f32[2,512]{1,0:T(2,128)S(1)}, u32[]{:S(2)}, u32[]{:S(2)}) %collective-permute-start.7) | collective-permute-done | bytes 4128 | tf_op jit(solution)/shard_map/ppermute | solution.py:90
  25.6 3.5 %collective-permute-start.8 = (f32[2,512]{1,0:T(2,128)S(1)}, f32[2,512]{1,0:T(2,128)S(1)}, u32[]{:S(2)}, u32[]{:S(2)}) collective-permute-start(f32[2,512]{1,0:T(2,128)S(1)} %get-tuple-element.55), channel_id=1, source_target_pairs={{0,0},{1,2},{2,1},{3,3},{4,4},{5,6},{6,5},{7,7},{8,8},{9,10},{10,9... | collective-permute-start | bytes 12296 | tf_op jit(solution)/shard_map/ppermute | solution.py:90
  29.1 1.2 %shard_map.127 = (f32[16,128]{1,0:T(8,128)S(1)}, bf16[512,2048]{1,0:T(8,128)(2,1)S(1)}) custom-call(f32[16,32,128]{2,1,0:T(8,128)S(1)} %get-tuple-element.45.t_ref.refs_10_, s32[32,128]{1,0:T(8,128)S(1)} %get-tuple-element.46.hv_ref.refs_6_, f32[32,128]{1,0:T(8,128)S(1)} %get-tuple-element.47.liq_ref, f32[32,128]{1,0:T(8,128)S(1)} %get-tuple-element.48.tf_ref), custom_call_target="tpu_custom_call" | custom-call | tf_op jit(solution)/shard_map/pallas_call | solution.py:22
  30.3 1.2 %shard_map.126 = (f32[16,128]{1,0:T(8,128)S(1)}, bf16[512,2048]{1,0:T(8,128)(2,1)S(1)}) custom-call(f32[16,32,128]{2,1,0:T(8,128)S(1)} %get-tuple-element.45.t_ref.refs_10_, s32[32,128]{1,0:T(8,128)S(1)} %get-tuple-element.46.hv_ref.refs_6_, f32[32,128]{1,0:T(8,128)S(1)} %get-tuple-element.47.liq_ref, f32[32,128]{1,0:T(8,128)S(1)} %get-tuple-element.48.tf_ref), custom_call_target="tpu_custom_call" | custom-call | tf_op jit(solution)/shard_map/pallas_call | solution.py:22
  31.5 0.0 collective-permute-done.8.rest_1_
  31.5 0.8 %shard_map.128 = (f32[16,32,128]{2,1,0:T(8,128)S(1)}, f32[16,32,128]{2,1,0:T(8,128)S(1)}, f32[16,32,128]{2,1,0:T(8,128)S(1)}) custom-call(f32[16,32,128]{2,1,0:T(8,128)S(1)} %get-tuple-element.45.t_ref.refs_10_, f32[16,32,128]{2,1,0:T(8,128)S(1)} %get-tuple-element.53.c_ref.refs_11_, f32[2,512]{1,0:T(2,128)S(1)} %collective-permute-done.7.rest_0_, ...), custom_call_target="tpu_custom_call" | custom-call | tf_op jit(solution)/shard_map/pallas_call | solution.py:22
  32.3 0.6 %shard_map.125.refs_3_ = f32[32,128]{1,0:T(8,128)S(1)} custom-call(bf16[32,128,128]{2,1,0:T(8,128)(2,1)S(1)} %get-tuple-element.38.a_ref, f32[32,128]{1,0:T(8,128)S(1)} %get-tuple-element.44.h_ref.refs_12_), custom_call_target="tpu_custom_call" | custom-call | tf_op jit(solution)/shard_map/pallas_call | solution.py:22
  33.0 0.0 collective-permute-done.15.refs_19_
  33.0 0.0 collective-permute-done.10.refs_14_
  33.0 0.0 collective-permute-done.11.refs_15_
  33.0 0.0 collective-permute-done.14.refs_18_
  33.0 3.4 %shard_map.129 = (f32[32,128]{1,0:T(8,128)}, f32[16,32,128]{2,1,0:T(8,128)S(1)}, f32[16,32,128]{2,1,0:T(8,128)S(1)}, f32[2,32,128]{2,1,0:T(8,128)S(1)}, f32[2,16...) custom-call(f32[256,128]{1,0:T(8,128)S(1)} %get-tuple-element.43.ref, ...), custom_call_target="tpu_custom_call" | custom-call | tf_op jit(solution)/shard_map/pallas_call | solution.py:22
  36.4 0.0 collective-permute-start.16
  36.4 2.5 %collective-permute-start.17 = (f32[1,32,128]{2,1,0:T(8,128)S(1)}, f32[1,32,128]{2,1,0:T(8,128)S(1)}, u32[]{:S(2)}, u32[]{:S(2)}) collective-permute-start(f32[1,32,128]{2,1,0:T(8,128)S(1)} %get-tuple-element.68), channel_id=1, source_target_pairs={{0,0},{8,16},{16,8},{24,24},{1,1},{9,17},{17,9},{25,25},{2,2},{10,... | collective-permute-start | bytes 49160 | tf_op jit(solution)/shard_map/ppermute | solution.py:90
  38.9 0.6 %collective-permute-start.18 = (f32[1,16,128]{2,1,0:T(8,128)S(1)}, f32[1,16,128]{2,1,0:T(8,128)S(1)}, u32[]{:S(2)}, u32[]{:S(2)}) collective-permute-start(f32[1,16,128]{2,1,0:T(8,128)S(1)} %get-tuple-element.69), channel_id=1, source_target_pairs={{0,4},{4,0},{1,5},{5,1},{2,6},{6,2},{3,7},{7,3},{8,12},{12,8},{9,1... | collective-permute-start | bytes 24584 | tf_op jit(solution)/shard_map/ppermute | solution.py:90
  39.5 0.0 collective-permute-start.19
  39.6 3.0 %collective-permute-start.20 = (f32[1,512]{1,0:T(1,128)S(1)}, f32[1,512]{1,0:T(1,128)S(1)}, u32[]{:S(2)}, u32[]{:S(2)}) collective-permute-start(f32[1,512]{1,0:T(1,128)S(1)} %get-tuple-element.71), channel_id=1, source_target_pairs={{0,0},{1,2},{2,1},{3,3},{4,4},{5,6},{6,5},{7,7},{8,8},{9,10},{10,9... | collective-permute-start | bytes 6152 | tf_op jit(solution)/shard_map/ppermute | solution.py:90
  42.6 0.4 shard_map.130.v_ref
  43.0 0.1 collective-permute-done.19.rest_3_
  43.1 1.9 %collective-permute-done.20.rest_4_ = f32[1,512]{1,0:T(1,128)S(1)} collective-permute-done((f32[1,512]{1,0:T(1,128)S(1)}, f32[1,512]{1,0:T(1,128)S(1)}, u32[]{:S(2)}, u32[]{:S(2)}) %collective-permute-start.20) | collective-permute-done | bytes 2080 | tf_op jit(solution)/shard_map/ppermute | solution.py:90
  45.0 0.0 collective-permute-done.18.rest_2_
  45.0 0.0 collective-permute-done.16.rest_0_
  45.0 0.0 collective-permute-done.17.rest_1_
  45.0 1.2 %shard_map.131 = f32[16,32,128]{2,1,0:T(8,128)} custom-call(f32[16,32,128]{2,1,0:T(8,128)S(1)} %shard_map.130.v_ref, f32[16,32,128]{2,1,0:T(8,128)S(1)} %get-tuple-element.61.t_ref, f32[2,32,128]{2,1,0:T(8,128)S(1)} %get-tuple-element.64.wx_ref, f32[2,16,128]{2,1,0:T(8,128)S(1)} %get-tuple-element.65.wy_ref, f32[16,32,128]{2,1,0:T(8,128)S(1)} %get-tuple-element.66.wz_ref, ...), custom_call_target="tpu_custom_call" | custom-call | tf_op jit(solution)/shard_map/pallas_call | solution.py:22
  (1 shorter events, 0.0 us)
Async XLA Ops:
  2.7 5.4 %collective-permute-start.4 = (f32[104,128]{1,0:T(8,128)S(1)}, f32[104,128]{1,0:T(8,128)S(1)}, u32[]{:S(2)}, u32[]{:S(2)}) collective-permute-start(f32[104,128]{1,0:T(8,128)S(1)} %get-tuple-element.39.rest_0_), channel_id=1, source_target_pairs={{0,20},{4,16},{8,28},{12,24},{16,4},{20,0},{24,12},{28,8},{1,21},{... | collective-permute-start | bytes 159752 | tf_op jit(solution)/shard_map/ppermute | solution.py:55
  4.2 4.3 %collective-permute-start.3 = (f32[104,128]{1,0:T(8,128)S(1)}, f32[104,128]{1,0:T(8,128)S(1)}, u32[]{:S(2)}, u32[]{:S(2)}) collective-permute-start(f32[104,128]{1,0:T(8,128)S(1)} %get-tuple-element.39.rest_0_), channel_id=1, source_target_pairs={{0,16},{4,20},{8,24},{12,28},{16,0},{20,4},{24,8},{28,12},{1,17},{... | collective-permute-start | bytes 159752 | tf_op jit(solution)/shard_map/ppermute | solution.py:55
  5.7 4.1 %collective-permute-start = (f32[104,128]{1,0:T(8,128)S(1)}, f32[104,128]{1,0:T(8,128)S(1)}, u32[]{:S(2)}, u32[]{:S(2)}) collective-permute-start(f32[104,128]{1,0:T(8,128)S(1)} %get-tuple-element.39.rest_0_), channel_id=1, source_target_pairs={{0,4},{4,0},{8,12},{12,8},{16,20},{20,16},{24,28},{28,24},{1,5},{5... | collective-permute-start | bytes 159752 | tf_op jit(solution)/shard_map/ppermute | solution.py:55
  6.2 5.6 %collective-permute-start.1 = (f32[104,128]{1,0:T(8,128)S(1)}, f32[104,128]{1,0:T(8,128)S(1)}, u32[]{:S(2)}, u32[]{:S(2)}) collective-permute-start(f32[104,128]{1,0:T(8,128)S(1)} %get-tuple-element.39.rest_0_), channel_id=1, source_target_pairs={{0,8},{4,12},{8,0},{12,4},{16,24},{20,28},{24,16},{28,20},{1,9},{5... | collective-permute-start | bytes 159752 | tf_op jit(solution)/shard_map/ppermute | solution.py:55
  8.0 3.8 %collective-permute-start.6 = (f32[104,128]{1,0:T(8,128)S(1)}, f32[104,128]{1,0:T(8,128)S(1)}, u32[]{:S(2)}, u32[]{:S(2)}) collective-permute-start(f32[104,128]{1,0:T(8,128)S(1)} %collective-permute-done.4.rest_5_), channel_id=1, source_target_pairs={{0,8},{4,12},{8,0},{12,4},{16,24},{20,28},{24,16},{28,20},{1,9},{5... | collective-permute-start | bytes 159752 | tf_op jit(solution)/shard_map/ppermute | solution.py:55
  8.4 3.4 %collective-permute-start.5 = (f32[104,128]{1,0:T(8,128)S(1)}, f32[104,128]{1,0:T(8,128)S(1)}, u32[]{:S(2)}, u32[]{:S(2)}) collective-permute-start(f32[104,128]{1,0:T(8,128)S(1)} %collective-permute-done.3.rest_4_), channel_id=1, source_target_pairs={{0,8},{4,12},{8,0},{12,4},{16,24},{20,28},{24,16},{28,20},{1,9},{5... | collective-permute-start | bytes 159752 | tf_op jit(solution)/shard_map/ppermute | solution.py:55
  9.8 2.1 %collective-permute-start.2 = (f32[104,128]{1,0:T(8,128)S(1)}, f32[104,128]{1,0:T(8,128)S(1)}, u32[]{:S(2)}, u32[]{:S(2)}) collective-permute-start(f32[104,128]{1,0:T(8,128)S(1)} %collective-permute-done.rest_1_), channel_id=1, source_target_pairs={{0,8},{4,12},{8,0},{12,4},{16,24},{20,28},{24,16},{28,20},{1,9},{5... | collective-permute-start | bytes 159752 | tf_op jit(solution)/shard_map/ppermute | solution.py:55
  13.1 4.2 %collective-permute-start.12 = (f32[96,128]{1,0:T(8,128)S(1)}, f32[96,128]{1,0:T(8,128)S(1)}, u32[]{:S(2)}, u32[]{:S(2)}) collective-permute-start(f32[96,128]{1,0:T(8,128)S(1)} %get-tuple-element.59), channel_id=1, source_target_pairs={{0,16},{4,20},{8,24},{12,28},{16,0},{20,4},{24,8},{28,12},{1,17},{... | collective-permute-start | bytes 147464 | tf_op jit(solution)/shard_map/ppermute | solution.py:55
  13.7 4.2 %collective-permute-start.9 = (f32[64,128]{1,0:T(8,128)S(1)}, f32[64,128]{1,0:T(8,128)S(1)}, u32[]{:S(2)}, u32[]{:S(2)}) collective-permute-start(f32[64,128]{1,0:T(8,128)S(1)} %get-tuple-element.57), channel_id=1, source_target_pairs={{0,4},{4,0},{8,12},{12,8},{16,20},{20,16},{24,28},{28,24},{1,5},{5... | collective-permute-start | bytes 98312 | tf_op jit(solution)/shard_map/ppermute | solution.py:55
  14.3 18.6 %collective-permute-start.10 = (f32[96,128]{1,0:T(8,128)S(1)}, f32[96,128]{1,0:T(8,128)S(1)}, u32[]{:S(2)}, u32[]{:S(2)}) collective-permute-start(f32[96,128]{1,0:T(8,128)S(1)} %get-tuple-element.58), channel_id=1, source_target_pairs={{0,8},{4,12},{8,0},{12,4},{16,24},{20,28},{24,16},{28,20},{1,9},{5... | collective-permute-start | bytes 147464 | tf_op jit(solution)/shard_map/ppermute | solution.py:55
  17.4 15.7 %collective-permute-start.14 = (f32[96,128]{1,0:T(8,128)S(1)}, f32[96,128]{1,0:T(8,128)S(1)}, u32[]{:S(2)}, u32[]{:S(2)}) collective-permute-start(f32[96,128]{1,0:T(8,128)S(1)} %collective-permute-done.12.refs_16_), channel_id=1, source_target_pairs={{0,8},{4,12},{8,0},{12,4},{16,24},{20,28},{24,16},{28,20},{1,9},{5... | collective-permute-start | bytes 147464 | tf_op jit(solution)/shard_map/ppermute | solution.py:55
  17.4 4.6 %collective-permute-start.13 = (f32[32,128]{1,0:T(8,128)S(1)}, f32[32,128]{1,0:T(8,128)S(1)}, u32[]{:S(2)}, u32[]{:S(2)}) collective-permute-start(f32[32,128]{1,0:T(8,128)S(1)} %get-tuple-element.44.h_ref.refs_12_), channel_id=1, source_target_pairs={{0,20},{4,16},{8,28},{12,24},{16,4},{20,0},{24,12},{28,8},{1,21},{... | collective-permute-start | bytes 49160 | tf_op jit(solution)/shard_map/ppermute | solution.py:55
  17.9 15.1 %collective-permute-start.11 = (f32[64,128]{1,0:T(8,128)S(1)}, f32[64,128]{1,0:T(8,128)S(1)}, u32[]{:S(2)}, u32[]{:S(2)}) collective-permute-start(f32[64,128]{1,0:T(8,128)S(1)} %collective-permute-done.9.refs_13_), channel_id=1, source_target_pairs={{0,8},{4,12},{8,0},{12,4},{16,24},{20,28},{24,16},{28,20},{1,9},{5... | collective-permute-start | bytes 98312 | tf_op jit(solution)/shard_map/ppermute | solution.py:55
  22.0 11.0 %collective-permute-start.15 = (f32[32,128]{1,0:T(8,128)S(1)}, f32[32,128]{1,0:T(8,128)S(1)}, u32[]{:S(2)}, u32[]{:S(2)}) collective-permute-start(f32[32,128]{1,0:T(8,128)S(1)} %collective-permute-done.13.refs_17_), channel_id=1, source_target_pairs={{0,8},{4,12},{8,0},{12,4},{16,24},{20,28},{24,16},{28,20},{1,9},{5... | collective-permute-start | bytes 49160 | tf_op jit(solution)/shard_map/ppermute | solution.py:55
  22.0 3.6 %collective-permute-start.7 = (f32[2,512]{1,0:T(2,128)S(1)}, f32[2,512]{1,0:T(2,128)S(1)}, u32[]{:S(2)}, u32[]{:S(2)}) collective-permute-start(f32[2,512]{1,0:T(2,128)S(1)} %get-tuple-element.54), channel_id=1, source_target_pairs={{0,1},{1,0},{2,3},{3,2},{4,5},{5,4},{6,7},{7,6},{8,9},{9,8},{10,11... | collective-permute-start | bytes 12296 | tf_op jit(solution)/shard_map/ppermute | solution.py:90
  25.6 5.9 %collective-permute-start.8 = (f32[2,512]{1,0:T(2,128)S(1)}, f32[2,512]{1,0:T(2,128)S(1)}, u32[]{:S(2)}, u32[]{:S(2)}) collective-permute-start(f32[2,512]{1,0:T(2,128)S(1)} %get-tuple-element.55), channel_id=1, source_target_pairs={{0,0},{1,2},{2,1},{3,3},{4,4},{5,6},{6,5},{7,7},{8,8},{9,10},{10,9... | collective-permute-start | bytes 12296 | tf_op jit(solution)/shard_map/ppermute | solution.py:90
  36.4 8.6 %collective-permute-start.16 = (f32[1,32,128]{2,1,0:T(8,128)S(1)}, f32[1,32,128]{2,1,0:T(8,128)S(1)}, u32[]{:S(2)}, u32[]{:S(2)}) collective-permute-start(f32[1,32,128]{2,1,0:T(8,128)S(1)} %get-tuple-element.67), channel_id=1, source_target_pairs={{0,8},{8,0},{16,24},{24,16},{1,9},{9,1},{17,25},{25,17},{2,10},{10... | collective-permute-start | bytes 49160 | tf_op jit(solution)/shard_map/ppermute | solution.py:90
  36.4 8.6 %collective-permute-start.17 = (f32[1,32,128]{2,1,0:T(8,128)S(1)}, f32[1,32,128]{2,1,0:T(8,128)S(1)}, u32[]{:S(2)}, u32[]{:S(2)}) collective-permute-start(f32[1,32,128]{2,1,0:T(8,128)S(1)} %get-tuple-element.68), channel_id=1, source_target_pairs={{0,0},{8,16},{16,8},{24,24},{1,1},{9,17},{17,9},{25,25},{2,2},{10,... | collective-permute-start | bytes 49160 | tf_op jit(solution)/shard_map/ppermute | solution.py:90
  38.9 6.1 %collective-permute-start.18 = (f32[1,16,128]{2,1,0:T(8,128)S(1)}, f32[1,16,128]{2,1,0:T(8,128)S(1)}, u32[]{:S(2)}, u32[]{:S(2)}) collective-permute-start(f32[1,16,128]{2,1,0:T(8,128)S(1)} %get-tuple-element.69), channel_id=1, source_target_pairs={{0,4},{4,0},{1,5},{5,1},{2,6},{6,2},{3,7},{7,3},{8,12},{12,8},{9,1... | collective-permute-start | bytes 24584 | tf_op jit(solution)/shard_map/ppermute | solution.py:90
  39.5 3.6 %collective-permute-start.19 = (f32[1,512]{1,0:T(1,128)S(1)}, f32[1,512]{1,0:T(1,128)S(1)}, u32[]{:S(2)}, u32[]{:S(2)}) collective-permute-start(f32[1,512]{1,0:T(1,128)S(1)} %get-tuple-element.70), channel_id=1, source_target_pairs={{0,1},{1,0},{2,3},{3,2},{4,5},{5,4},{6,7},{7,6},{8,9},{9,8},{10,11... | collective-permute-start | bytes 6152 | tf_op jit(solution)/shard_map/ppermute | solution.py:90
  39.6 5.5 %collective-permute-start.20 = (f32[1,512]{1,0:T(1,128)S(1)}, f32[1,512]{1,0:T(1,128)S(1)}, u32[]{:S(2)}, u32[]{:S(2)}) collective-permute-start(f32[1,512]{1,0:T(1,128)S(1)} %get-tuple-element.71), channel_id=1, source_target_pairs={{0,0},{1,2},{2,1},{3,3},{4,4},{5,6},{6,5},{7,7},{8,8},{9,10},{10,9... | collective-permute-start | bytes 6152 | tf_op jit(solution)/shard_map/ppermute | solution.py:90
